TPU v7x, 32 devices: a whole 2x2x4 slice. The times are simulated.
32 devices in a mesh: groups: 2 (over y), span: 4 (over z), batch: 4 (over x, core).
Axes of the slice: x: 2, y: 2, z: 4, core: 2. Of those that a mesh axis runs over, the one named last changes fastest.
Arguments:
- embeddings: bfloat16 [8, 512, 768], P(('groups', 'batch'), 'span'), parts along dimension 0, may hold values from -3500 to 3500
- cluster_ids: int32 [8, 512], P(('groups', 'batch'), 'span'), parts along dimension 0, may hold values from 0 to 15, as said below
Outputs:
- nearest: float32 [8, 512], P(('groups', 'batch'), 'span'), parts along dimension 0
There are 2 independent parts, one for each index of `groups`. A program takes and returns all parts, laid end to end along the dimension named above; each array names one. Nothing has to cross between parts.
Inputs may be any that keep to these rules, and one draw needn't show every extreme that they name: `cluster_ids`: on one device at most 96 rows carry ids of one residue modulo 4; in every batch some residue has exactly 96 rows on every device of the span.
All inputs are finite; a program needn't handle non-finite values.
Results may differ from a plain program's by a relative error of at most 0.00061.
Values may be sent and summed in bfloat16 or wider, within the bound.
No kernel may reach another device: no remote copies, remote signals or barrier semaphores. Data moves between devices by JAX's collectives and lax.ppermute only.
A program may use at most 64 MiB of HBM per device.

v0:
```python
import math

import jax
import jax.numpy as jnp
from jax import lax
from jax.sharding import PartitionSpec as P


SPAN = "span"
BATCH = "batch"


def normalize(embeddings):
    values = embeddings.astype(jnp.float32)
    inverse = lax.rsqrt(jnp.mean(values * values, axis=-1, keepdims=True) + 1e-06)
    return (values * inverse * (1.0 / math.sqrt(values.shape[-1]))).astype(jnp.bfloat16)


def pair_scores(left, right):
    return lax.dot_general(
        left, right, (((1,), (1,)), ((), ())), preferred_element_type=jnp.float32
    )


def gathered(embeddings, cluster_ids):
    normed = normalize(embeddings[0])
    member_ids = cluster_ids[0]
    row_count = normed.shape[0]
    own_index = lax.axis_index(SPAN)
    own_rows = own_index * row_count + jnp.arange(row_count, dtype=jnp.int32)
    piece_rows = lax.all_gather(normed, SPAN, axis=0, tiled=True)
    piece_ids = lax.all_gather(member_ids.astype(jnp.bfloat16), SPAN, axis=0, tiled=True)
    scores = pair_scores(normed, piece_rows)
    column_rows = jnp.arange(piece_rows.shape[0], dtype=jnp.int32)
    same_cluster = (member_ids[:, None] == piece_ids.astype(jnp.int32)[None, :]) & (
        own_rows[:, None] != column_rows[None, :]
    )
    nearest = jnp.max(jnp.where(same_cluster, scores, -1.0), axis=1)
    return jnp.maximum(nearest, -1.0)[None, :]


TO_ROOT = (
    (("3e", "1e", "0e", "0o", "2o", "2e"), ("1o~",), ("3o~",)),
    (("2e", "1e", "1o", "2o"), ("0e", "0o"), ("3e", "3o")),
    (("0e", "1e", "1o", "0o"), ("3o", "2o", "2e", "3e")),
)
BACK = (
    (("1e", "0e", "0o", "1o"), ("2o", "3o", "3e", "2e")),
    (("1e", "3e", "2e", "2o", "0o", "0e"), ("1o~",), ("3o~",)),
    (("1e", "2e", "2o", "1o"), ("0e", "0o"), ("3e", "3o")),
)
MEET = (1, 2)
PLACES = 4


def following(cycles, spot):
    for stops in cycles:
        names = [stop[:2] for stop in stops]
        if spot in names:
            return names[(names.index(spot) + 1) % len(names)]


def wanted(place, parity):
    spot, root = f"{place}{'eo'[parity]}", f"{MEET[parity]}{'eo'[parity]}"
    if spot == root:
        return 0
    block = 1 + [following(cycles, spot) == root for cycles in TO_ROOT].index(True)
    source = 1 + [following(cycles, root) == spot for cycles in BACK].index(True)
    return source * PLACES + block


def pairs(cycles, batches):
    moves = {}
    for stops in cycles:
        for here, there in zip(stops, stops[1:] + stops[:1]):
            for low in range(0, batches, 2):
                spot = (int(here[0]), low + "eo".index(here[1]))
                other = low ^ 2 if here.endswith("~") else low
                moves[spot] = (int(there[0]), other + "eo".index(there[1]))
    flat = lambda spot: spot[0] * batches + spot[1]
    return sorted((flat(a), flat(b)) for a, b in moves.items())


def travel(array, cycles, batches):
    return lax.ppermute(array, (SPAN, BATCH), pairs(cycles, batches))


def at_root(batches):
    def per_device(embeddings, cluster_ids):
        return whole(embeddings, cluster_ids)

    def whole(embeddings, cluster_ids):
        rows = embeddings[0]
        row_count = rows.shape[0]
        arrived = [travel(rows, cycles, batches) for cycles in TO_ROOT]
        arrived_ids = [travel(cluster_ids, cycles, batches) for cycles in TO_ROOT]
        normed = jnp.concatenate([normalize(r) for r in [rows] + arrived], axis=0)
        ids = jnp.concatenate([cluster_ids] + arrived_ids, axis=1)[0]
        scores = pair_scores(normed, normed)
        index = jnp.arange(ids.shape[0], dtype=jnp.int32)
        keep = (ids[:, None] == ids[None, :]) & (index[:, None] != index[None, :])
        best = jnp.maximum(jnp.max(jnp.where(keep, scores, -1.0), axis=0), -1.0)
        best = best.reshape(-1, row_count)
        back = [travel(best, cycles, batches) for cycles in BACK]
        stack = jnp.concatenate([best] + back, axis=0)
        where_am_i = lax.axis_index(SPAN) * 2 + (lax.axis_index(BATCH) & 1)
        row = lax.broadcasted_iota(jnp.int32, stack.shape, 0)
        mine = jnp.zeros(stack.shape, jnp.bool_)
        for place in range(PLACES):
            for parity in range(2):
                here = where_am_i == place * 2 + parity
                mine |= here & (row == wanted(place, parity))
        return jnp.max(jnp.where(mine, stack, -1.0), axis=0)[None, :]

    return per_device


def solution(mesh):
    batches = mesh.shape[BATCH]
    line = mesh.shape[SPAN] == PLACES and batches % 4 == 0
    return jax.shard_map(
        at_root(batches) if line else gathered,
        mesh=mesh,
        in_specs=(P(("groups", BATCH), SPAN, None), P(("groups", BATCH), SPAN)),
        out_specs=P(("groups", BATCH), SPAN),
        check_vma=False,
    )
```

profile of v0, /device:TPU:0, one launch (start us, length us, event | category | flops | bytes accessed | tf_op | source)
XLA Modules:
  0.0 21.1 jit_solution(8831783855609635173)
XLA Ops:
  0.0 3.1 %collective-permute-start.5 = (bf16[128,768]{1,0:T(8,128)(2,1)}, bf16[128,768]{1,0:T(8,128)(2,1)S(1)}, u32[]{:S(2)}, u32[]{:S(2)}) collective-permute-start(bf16[128,768]{1,0:T(8,128)(2,1)} %bitcast.7), channel_id=1, source_target_pairs={{0,4},{1,0},{2,6},{3,2},{4,5},{5,1},{6,7},{7,3},{8,12},{9,8},{10,1... | collective-permute-start | bytes 589832 | tf_op jit(solution)/shard_map/ppermute | solution.py:85
  3.1 0.0 collective-permute-start.4
  3.1 0.1 collective-permute-start.2
  3.2 0.4 %collective-permute-start.1 = (s32[1,128]{1,0:T(1,128)}, s32[1,128]{1,0:T(1,128)S(1)}, u32[]{:S(2)}, u32[]{:S(2)}) collective-permute-start(s32[1,128]{1,0:T(1,128)} %param.3), channel_id=1, source_target_pairs={{0,1},{1,0},{2,3},{3,2},{4,5},{5,9},{6,7},{7,11},{8,4},{9,8},{10,6... | collective-permute-start | bytes 1544 | tf_op jit(solution)/shard_map/ppermute | solution.py:85
  3.6 0.1 collective-permute-start
  3.7 1.0 %fusion.9 = f32[128]{0:T(128)S(1)} fusion(bf16[1,128,768]{2,1,0:T(8,128)(2,1)} %param.2), kind=kLoop, calls=%fused_computation.19 | loop fusion | flops 294784 | bytes 197120 | tf_op jit(solution)/shard_map/reduce_sum | solution.py:15
  4.8 0.0 copy-start.1
  4.8 0.1 fusion.11
  4.9 1.7 %collective-permute-done.2 = s32[1,128]{1,0:T(1,128)S(1)} collective-permute-done((s32[1,128]{1,0:T(1,128)}, s32[1,128]{1,0:T(1,128)S(1)}, u32[]{:S(2)}, u32[]{:S(2)}) %collective-permute-start.2) | collective-permute-done | bytes 544 | tf_op jit(solution)/shard_map/ppermute | solution.py:85
  6.6 0.7 %collective-permute-start.3 = (bf16[128,768]{1,0:T(8,128)(2,1)S(1)}, bf16[128,768]{1,0:T(8,128)(2,1)S(1)}, u32[]{:S(2)}, u32[]{:S(2)}) collective-permute-start(bf16[128,768]{1,0:T(8,128)(2,1)S(1)} %bitcast.9), channel_id=1, source_target_pairs={{0,1},{1,9},{2,3},{3,11},{4,0},{5,7},{6,2},{7,5},{8,12},{9,8},{10,... | collective-permute-start | bytes 589832 | tf_op jit(solution)/shard_map/ppermute | solution.py:85
  7.3 0.0 collective-permute-done.1
  7.3 0.1 fusion.18
  7.5 0.1 fusion.15
  7.6 5.1 %collective-permute-done.3 = bf16[128,768]{1,0:T(8,128)(2,1)S(1)} collective-permute-done((bf16[128,768]{1,0:T(8,128)(2,1)S(1)}, bf16[128,768]{1,0:T(8,128)(2,1)S(1)}, u32[]{:S(2)}, u32[]{:S(2)}) %collective-permute-start.3) | collective-permute-done | bytes 196640 | tf_op jit(solution)/shard_map/ppermute | solution.py:85
  12.7 0.1 fusion.12
  12.8 0.1 fusion.20
  12.9 0.1 fusion.17
  13.0 0.1 fusion.14
  13.2 0.7 %fusion = f32[512]{0:T(512)S(1)} fusion(bf16[128,768]{1,0:T(8,128)(2,1)S(1)} %fusion.20, bf16[128,768]{1,0:T(8,128)(2,1)S(1)} %fusion.17, bf16[128,768]{1,0:T(8,128)(2,1)S(1)} %fusion.14, bf16[128,768]{1,0:T(8,128)(2,1)S(1)} %fusion.11, s32[512]{0:T(512)S(1)} %bitcast.10), kind=kOutput, calls=%fused_computation.1 | convolution fusion | flops 407109120 | bytes 790528 | tf_op jit(solution)/shard_map/dot_general | solution.py:20
  13.9 0.1 collective-permute-start.8
  13.9 3.0 %collective-permute-start.7 = (f32[4,128]{1,0:T(4,128)S(1)}, f32[4,128]{1,0:T(4,128)S(1)}, u32[]{:S(2)}, u32[]{:S(2)}) collective-permute-start(f32[4,128]{1,0:T(4,128)S(1)} %maximum_bitcast_fusion), channel_id=1, source_target_pairs={{0,4},{1,0},{2,6},{3,2},{4,12},{5,7},{6,14},{7,5},{8,9},{9,1},{10,... | collective-permute-start | bytes 6152 | tf_op jit(solution)/shard_map/ppermute | solution.py:85
  16.9 1.3 %collective-permute-done.7 = f32[4,128]{1,0:T(4,128)S(1)} collective-permute-done((f32[4,128]{1,0:T(4,128)S(1)}, f32[4,128]{1,0:T(4,128)S(1)}, u32[]{:S(2)}, u32[]{:S(2)}) %collective-permute-start.7) | collective-permute-done | bytes 2080 | tf_op jit(solution)/shard_map/ppermute | solution.py:85
  18.2 2.3 %collective-permute-done.6 = f32[4,128]{1,0:T(4,128)S(1)} collective-permute-done((f32[4,128]{1,0:T(4,128)S(1)}, f32[4,128]{1,0:T(4,128)S(1)}, u32[]{:S(2)}, u32[]{:S(2)}) %collective-permute-start.6) | collective-permute-done | bytes 2080 | tf_op jit(solution)/shard_map/ppermute | solution.py:85
  20.5 0.6 %fusion.21 = f32[128]{0:T(128)} fusion(f32[4,128]{1,0:T(4,128)S(1)} %collective-permute-done.8, f32[4,128]{1,0:T(4,128)S(1)} %collective-permute-done.7, f32[4,128]{1,0:T(4,128)S(1)} %collective-permute-done.6, f32[4,128]{1,0:T(4,128)S(1)} %maximum_bitcast_fusion, pred[16]{0:T(512)(128)(4,1)S(1)} %and_or_fusion), kind=kLoop, calls=%fused_computation.32 | loop fusion | flops 10112 | bytes 8720 | tf_op jit(solution)/shard_map/reduce_max | solution.py:113
  (15 shorter events, 0.1 us)
Async XLA Ops:
  0.0 4.7 %copy-start = (bf16[1,128,768]{2,1,0:T(8,128)(2,1)S(1)}, bf16[1,128,768]{2,1,0:T(8,128)(2,1)}, u32[]{:S(2)}) copy-start(bf16[1,128,768]{2,1,0:T(8,128)(2,1)} %param.2) | copy-start | bytes 589828
  0.0 7.3 %collective-permute-start.5 = (bf16[128,768]{1,0:T(8,128)(2,1)}, bf16[128,768]{1,0:T(8,128)(2,1)S(1)}, u32[]{:S(2)}, u32[]{:S(2)}) collective-permute-start(bf16[128,768]{1,0:T(8,128)(2,1)} %bitcast.7), channel_id=1, source_target_pairs={{0,4},{1,0},{2,6},{3,2},{4,5},{5,1},{6,7},{7,3},{8,12},{9,8},{10,1... | collective-permute-start | bytes 589832 | tf_op jit(solution)/shard_map/ppermute | solution.py:85
  3.1 4.4 %collective-permute-start.4 = (bf16[128,768]{1,0:T(8,128)(2,1)}, bf16[128,768]{1,0:T(8,128)(2,1)S(1)}, u32[]{:S(2)}, u32[]{:S(2)}) collective-permute-start(bf16[128,768]{1,0:T(8,128)(2,1)} %bitcast.8), channel_id=1, source_target_pairs={{0,1},{1,0},{2,3},{3,2},{4,5},{5,9},{6,7},{7,11},{8,4},{9,8},{10,6... | collective-permute-start | bytes 589832 | tf_op jit(solution)/shard_map/ppermute | solution.py:85
  3.1 3.5 %collective-permute-start.2 = (s32[1,128]{1,0:T(1,128)}, s32[1,128]{1,0:T(1,128)S(1)}, u32[]{:S(2)}, u32[]{:S(2)}) collective-permute-start(s32[1,128]{1,0:T(1,128)} %param.3), channel_id=1, source_target_pairs={{0,4},{1,0},{2,6},{3,2},{4,5},{5,1},{6,7},{7,3},{8,12},{9,8},{10,1... | collective-permute-start | bytes 1544 | tf_op jit(solution)/shard_map/ppermute | solution.py:85
  3.2 4.1 %collective-permute-start.1 = (s32[1,128]{1,0:T(1,128)}, s32[1,128]{1,0:T(1,128)S(1)}, u32[]{:S(2)}, u32[]{:S(2)}) collective-permute-start(s32[1,128]{1,0:T(1,128)} %param.3), channel_id=1, source_target_pairs={{0,1},{1,0},{2,3},{3,2},{4,5},{5,9},{6,7},{7,11},{8,4},{9,8},{10,6... | collective-permute-start | bytes 1544 | tf_op jit(solution)/shard_map/ppermute | solution.py:85
  3.6 3.7 %collective-permute-start = (s32[1,128]{1,0:T(1,128)}, s32[1,128]{1,0:T(1,128)S(1)}, u32[]{:S(2)}, u32[]{:S(2)}) collective-permute-start(s32[1,128]{1,0:T(1,128)} %param.3), channel_id=1, source_target_pairs={{0,1},{1,9},{2,3},{3,11},{4,0},{5,7},{6,2},{7,5},{8,12},{9,8},{10,... | collective-permute-start | bytes 1544 | tf_op jit(solution)/shard_map/ppermute | solution.py:85
  4.8 2.5 %copy-start.1 = (s32[1,128]{1,0:T(1,128)S(1)}, s32[1,128]{1,0:T(1,128)}, u32[]{:S(2)}) copy-start(s32[1,128]{1,0:T(1,128)} %param.3) | copy-start | bytes 1540
  6.6 6.1 %collective-permute-start.3 = (bf16[128,768]{1,0:T(8,128)(2,1)S(1)}, bf16[128,768]{1,0:T(8,128)(2,1)S(1)}, u32[]{:S(2)}, u32[]{:S(2)}) collective-permute-start(bf16[128,768]{1,0:T(8,128)(2,1)S(1)} %bitcast.9), channel_id=1, source_target_pairs={{0,1},{1,9},{2,3},{3,11},{4,0},{5,7},{6,2},{7,5},{8,12},{9,8},{10,... | collective-permute-start | bytes 589832 | tf_op jit(solution)/shard_map/ppermute | solution.py:85
  13.9 3.1 %collective-permute-start.8 = (f32[4,128]{1,0:T(4,128)S(1)}, f32[4,128]{1,0:T(4,128)S(1)}, u32[]{:S(2)}, u32[]{:S(2)}) collective-permute-start(f32[4,128]{1,0:T(4,128)S(1)} %maximum_bitcast_fusion), channel_id=1, source_target_pairs={{0,1},{1,0},{2,3},{3,2},{4,8},{5,4},{6,10},{7,6},{8,9},{9,5},{10,1... | collective-permute-start | bytes 6152 | tf_op jit(solution)/shard_map/ppermute | solution.py:85
  13.9 4.3 %collective-permute-start.7 = (f32[4,128]{1,0:T(4,128)S(1)}, f32[4,128]{1,0:T(4,128)S(1)}, u32[]{:S(2)}, u32[]{:S(2)}) collective-permute-start(f32[4,128]{1,0:T(4,128)S(1)} %maximum_bitcast_fusion), channel_id=1, source_target_pairs={{0,4},{1,0},{2,6},{3,2},{4,12},{5,7},{6,14},{7,5},{8,9},{9,1},{10,... | collective-permute-start | bytes 6152 | tf_op jit(solution)/shard_map/ppermute | solution.py:85
  16.9 3.6 %collective-permute-start.6 = (f32[4,128]{1,0:T(4,128)S(1)}, f32[4,128]{1,0:T(4,128)S(1)}, u32[]{:S(2)}, u32[]{:S(2)}) collective-permute-start(f32[4,128]{1,0:T(4,128)S(1)} %maximum_bitcast_fusion), channel_id=1, source_target_pairs={{0,1},{1,5},{2,3},{3,7},{4,0},{5,4},{6,2},{7,6},{8,9},{9,13},{10,1... | collective-permute-start | bytes 6152 | tf_op jit(solution)/shard_map/ppermute | solution.py:85
where the time goes:
time: 21.2 us; the launch traced here: 21.1 us
  waiting for transfers between devices  10.3 us (49%)
  starting transfers between devices  7.46 us (35%)
  other arithmetic  2.51 us (12%)
  matrix products  0.68 us (3%)
    ppermute x9, waiting for transfers between devices, travel(): return lax.ppermute(array, (SPAN, BATCH), pairs(cycles, batches))  10.3 us
    ppermute x9, starting transfers between devices, travel(): return lax.ppermute(array, (SPAN, BATCH), pairs(cycles, batches))  7.46 us
    reduce_sum x4, other arithmetic, normalize(): jnp.mean(values * values, axis=-1, keepdims=True) + 1e-06  1.41 us
    dot_general x1, matrix products, pair_scores(): lax.dot_general(left, right, (((1,), (1,)), ((), ())), preferred_element_...  0.68 us
    reduce_max x1, other arithmetic, whole(): return jnp.max(jnp.where(mine, stack, -1.0), axis=0)[None, :]  0.6 us
    convert_element_type x4, other arithmetic, normalize(): (values * inverse * (1.0 / math.sqrt(values.shape[-1]))).astype(jnp.bfloa...  0.45 us
  transfers between devices with their start and end apart: 9, of which 4 were waited for; matrix products, arithmetic and copies ran while one was open for 7% of the time, Pallas kernels for 0%

commit v1 on v0

--- a/solution.py
+++ b/solution.py
@@ -3,6 +3,8 @@
 import jax
 import jax.numpy as jnp
 from jax import lax
+from jax.experimental import pallas as pl
+from jax.experimental.pallas import tpu as pltpu
 from jax.sharding import PartitionSpec as P
 
 
@@ -40,8 +42,8 @@
 
 
 TO_ROOT = (
-    (("3e", "1e", "0e", "0o", "2o", "2e"), ("1o~",), ("3o~",)),
     (("2e", "1e", "1o", "2o"), ("0e", "0o"), ("3e", "3o")),
+    (("3e", "1e", "0e", "0o", "2o", "3o"), ("1o~",), ("2e~",)),
     (("0e", "1e", "1o", "0o"), ("3o", "2o", "2e", "3e")),
 )
 BACK = (
@@ -85,22 +87,61 @@
     return lax.ppermute(array, (SPAN, BATCH), pairs(cycles, batches))
 
 
+GRANT = pltpu.CompilerParams(vmem_limit_bytes=8 << 20)
+WHOLE = pl.BlockSpec(memory_space=pltpu.VMEM)
+
+
+def own_body(rows, out):
+    out[...] = normalize(rows[...])
+
+
+def root_body(own, *refs):
+    n = PLACES
+    arrived, ids, out = refs[: n - 1], refs[n - 1 : 2 * n - 1], refs[2 * n - 1]
+    count = own.shape[0]
+    normed = jnp.concatenate([own[...]] + [normalize(r[...]) for r in arrived], axis=0)
+    across = jnp.concatenate([i[...] for i in ids], axis=1)
+    index = lax.broadcasted_iota(jnp.int32, (1, across.shape[1]), 1)
+    down = jnp.transpose(jnp.broadcast_to(across, (8, across.shape[1])))[:, :1]
+    down_index = lax.broadcasted_iota(jnp.int32, (down.shape[0], 1), 0)
+    scores = pair_scores(normed, normed)
+    keep = (down == across) & (down_index != index)
+    best = jnp.maximum(jnp.max(jnp.where(keep, scores, -1.0), axis=0, keepdims=True), -1.0)
+    for k in range(n):
+        out[k : k + 1, :] = best[:, k * count : (k + 1) * count]
+
+
+def own_rows(rows):
+    return pl.pallas_call(
+        own_body,
+        out_shape=jax.ShapeDtypeStruct(rows.shape, jnp.bfloat16),
+        in_specs=[WHOLE],
+        out_specs=WHOLE,
+        compiler_params=GRANT,
+        name="own_rows",
+    )(rows)
+
+
+def all_results(own, arrived, ids):
+    return pl.pallas_call(
+        root_body,
+        out_shape=jax.ShapeDtypeStruct((PLACES, own.shape[0]), jnp.float32),
+        in_specs=[WHOLE] * (2 * PLACES),
+        out_specs=WHOLE,
+        compiler_params=GRANT,
+        name="all_results",
+    )(own, *arrived, *ids)
+
+
 def at_root(batches):
     def per_device(embeddings, cluster_ids):
         return whole(embeddings, cluster_ids)
 
     def whole(embeddings, cluster_ids):
         rows = embeddings[0]
-        row_count = rows.shape[0]
         arrived = [travel(rows, cycles, batches) for cycles in TO_ROOT]
         arrived_ids = [travel(cluster_ids, cycles, batches) for cycles in TO_ROOT]
-        normed = jnp.concatenate([normalize(r) for r in [rows] + arrived], axis=0)
-        ids = jnp.concatenate([cluster_ids] + arrived_ids, axis=1)[0]
-        scores = pair_scores(normed, normed)
-        index = jnp.arange(ids.shape[0], dtype=jnp.int32)
-        keep = (ids[:, None] == ids[None, :]) & (index[:, None] != index[None, :])
-        best = jnp.maximum(jnp.max(jnp.where(keep, scores, -1.0), axis=0), -1.0)
-        best = best.reshape(-1, row_count)
+        best = all_results(own_rows(rows), arrived, [cluster_ids] + arrived_ids)
         back = [travel(best, cycles, batches) for cycles in BACK]
         stack = jnp.concatenate([best] + back, axis=0)
         where_am_i = lax.axis_index(SPAN) * 2 + (lax.axis_index(BATCH) & 1)

time: 21.2 us -> 19.9 us (0.939)
  waiting for transfers between devices: 10.3 us -> 4.86 us
  starting transfers between devices: 7.46 us -> 12.4 us
  other arithmetic: 2.51 us -> 0.61 us
  Pallas kernels: 0 us -> 0.95 us
  local copies, waits for them, and re-layouts: 0.01 us -> 0.93 us
  matrix products: 0.68 us -> 0 us
    ppermute x9, waiting for transfers between devices: 10.3 us -> 4.86 us  [travel(): return lax.ppermute(array, (SPAN, BATCH), pairs(cycles, batches))]
    ppermute x9, starting transfers between devices: 7.46 us -> 12.4 us  [travel(): return lax.ppermute(array, (SPAN, BATCH), pairs(cycles, batches))]
    reduce_sum x4 -> x0, other arithmetic: 1.41 us -> none  [normalize(): jnp.mean(values * values, axis=-1, keepdims=True) + 1e-06]
    pallas_call x0 -> x2, Pallas kernels: none -> 0.95 us  [the longest x1 0.81 us: all_results(): pl.pallas_call(root_body, out_shape=jax.ShapeDtypeStruct((PLACES, own.sha...]
    unnamed x4, local copies, waits for them, and re-layouts: 0.01 us -> 0.93 us
    dot_general x1 -> x0, matrix products: 0.68 us -> none  [pair_scores(): lax.dot_general(left, right, (((1,), (1,)), ((), ())), preferred_element_...]
    convert_element_type x4 -> x0, other arithmetic: 0.45 us -> none  [normalize(): (values * inverse * (1.0 / math.sqrt(values.shape[-1]))).astype(jnp.bfloa...]
  transfers between devices with their start and end apart: 9 -> 9, of which waited for: 4 -> 3; matrix products, arithmetic and copies ran while one was open for 7% -> 0% of each run, Pallas kernels for 0% -> 1%
where the time goes in v1:
time: 19.9 us; the launch traced here: 19.8 us
  starting transfers between devices  12.4 us (62%)
  waiting for transfers between devices  4.86 us (24%)
  Pallas kernels  0.95 us (5%)
  local copies, waits for them, and re-layouts  0.93 us (5%)
  other arithmetic  0.61 us (3%)
    ppermute x9, starting transfers between devices, travel(): return lax.ppermute(array, (SPAN, BATCH), pairs(cycles, batches))  12.4 us
    ppermute x9, waiting for transfers between devices, travel(): return lax.ppermute(array, (SPAN, BATCH), pairs(cycles, batches))  4.86 us
    unnamed x4, local copies, waits for them, and re-layouts  0.93 us
    pallas_call x1, Pallas kernels, all_results(): pl.pallas_call(root_body, out_shape=jax.ShapeDtypeStruct((PLACES, own.sha...  0.81 us
    reduce_max x1, other arithmetic, whole(): return jnp.max(jnp.where(mine, stack, -1.0), axis=0)[None, :]  0.6 us
  transfers between devices with their start and end apart: 9, of which 3 were waited for; matrix products, arithmetic and copies ran while one was open for 0% of the time, Pallas kernels for 1%

profile of v1, /device:TPU:0, one launch (start us, length us, event | category | flops | bytes accessed | tf_op | source)
XLA Modules:
  0.0 19.8 jit_solution(14888315436622168120)
XLA Ops:
  0.0 0.0 copy-start.1
  0.0 0.5 %collective-permute-start = (bf16[128,768]{1,0:T(8,128)(2,1)}, bf16[128,768]{1,0:T(8,128)(2,1)S(1)}, u32[]{:S(2)}, u32[]{:S(2)}) collective-permute-start(bf16[128,768]{1,0:T(8,128)(2,1)} %bitcast.2), channel_id=1, source_target_pairs={{0,1},{1,0},{2,3},{3,2},{4,5},{5,9},{6,7},{7,11},{8,4},{9,8},{10,6... | collective-permute-start | bytes 589832 | tf_op jit(solution)/shard_map/ppermute | solution.py:87
  0.5 0.1 collective-permute-start.1
  0.6 2.6 %collective-permute-start.2 = (bf16[128,768]{1,0:T(8,128)(2,1)}, bf16[128,768]{1,0:T(8,128)(2,1)S(1)}, u32[]{:S(2)}, u32[]{:S(2)}) collective-permute-start(bf16[128,768]{1,0:T(8,128)(2,1)} %bitcast.4), channel_id=1, source_target_pairs={{0,4},{1,0},{2,6},{3,2},{4,5},{5,1},{6,7},{7,3},{8,12},{9,8},{10,1... | collective-permute-start | bytes 589832 | tf_op jit(solution)/shard_map/ppermute | solution.py:87
  3.2 0.0 copy-done.1
  3.2 1.1 %collective-permute-start.3 = (s32[1,128]{1,0:T(1,128)S(1)}, s32[1,128]{1,0:T(1,128)S(1)}, u32[]{:S(2)}, u32[]{:S(2)}) collective-permute-start(s32[1,128]{1,0:T(1,128)S(1)} %copy-done.1), channel_id=1, source_target_pairs={{0,1},{1,0},{2,3},{3,2},{4,5},{5,9},{6,7},{7,11},{8,4},{9,8},{10,6... | collective-permute-start | bytes 1544 | tf_op jit(solution)/shard_map/ppermute | solution.py:87
  4.3 0.1 collective-permute-start.4
  4.4 0.9 %copy-done = bf16[1,128,768]{2,1,0:T(8,128)(2,1)S(1)} copy-done((bf16[1,128,768]{2,1,0:T(8,128)(2,1)S(1)}, bf16[1,128,768]{2,1,0:T(8,128)(2,1)}, u32[]{:S(2)}) %copy-start) | copy-done | bytes 196632
  5.3 0.1 own_rows.1.own
  5.4 0.0 collective-permute-done.3.refs_4_
  5.5 5.6 %collective-permute-start.5 = (s32[1,128]{1,0:T(1,128)S(1)}, s32[1,128]{1,0:T(1,128)S(1)}, u32[]{:S(2)}, u32[]{:S(2)}) collective-permute-start(s32[1,128]{1,0:T(1,128)S(1)} %copy-done.1), channel_id=1, source_target_pairs={{0,4},{1,0},{2,6},{3,2},{4,5},{5,1},{6,7},{7,3},{8,12},{9,8},{10,1... | collective-permute-start | bytes 1544 | tf_op jit(solution)/shard_map/ppermute | solution.py:87
  11.1 0.0 collective-permute-done.4.refs_5_
  11.1 1.3 %collective-permute-done.5.refs_6_ = s32[1,128]{1,0:T(1,128)S(1)} collective-permute-done((s32[1,128]{1,0:T(1,128)S(1)}, s32[1,128]{1,0:T(1,128)S(1)}, u32[]{:S(2)}, u32[]{:S(2)}) %collective-permute-start.5) | collective-permute-done | bytes 544 | tf_op jit(solution)/shard_map/ppermute | solution.py:87
  12.4 0.0 collective-permute-done.refs_0_
  12.4 0.0 collective-permute-done.1.refs_1_
  12.4 0.0 collective-permute-done.2.refs_2_
  12.4 0.8 %all_results.1 = f32[4,128]{1,0:T(4,128)S(1)} custom-call(bf16[128,768]{1,0:T(8,128)(2,1)S(1)} %own_rows.1.own, bf16[128,768]{1,0:T(8,128)(2,1)S(1)} %collective-permute-done.refs_0_, bf16[128,768]{1,0:T(8,128)(2,1)S(1)} %collective-permute-done.1.refs_1_, bf16[128,768]{1,0:T(8,128)(2,1)S(1)} %collective-permute-done.2.refs_2_, s32[1,128]{1,0:T(1,128)S(1)} %copy-done.1, ...), custom_call_target="tpu_custom_call" | custom-call | tf_op jit(solution)/shard_map/all_results/pallas_call | solution.py:126
  13.2 0.1 collective-permute-start.8
  13.3 2.3 %collective-permute-start.7 = (f32[4,128]{1,0:T(4,128)S(1)}, f32[4,128]{1,0:T(4,128)S(1)}, u32[]{:S(2)}, u32[]{:S(2)}) collective-permute-start(f32[4,128]{1,0:T(4,128)S(1)} %all_results.1), channel_id=1, source_target_pairs={{0,4},{1,0},{2,6},{3,2},{4,12},{5,7},{6,14},{7,5},{8,9},{9,1},{10,... | collective-permute-start | bytes 6152 | tf_op jit(solution)/shard_map/ppermute | solution.py:87
  15.6 0.0 collective-permute-start.6
  15.6 0.0 collective-permute-done.8
  15.6 1.3 %collective-permute-done.7 = f32[4,128]{1,0:T(4,128)S(1)} collective-permute-done((f32[4,128]{1,0:T(4,128)S(1)}, f32[4,128]{1,0:T(4,128)S(1)}, u32[]{:S(2)}, u32[]{:S(2)}) %collective-permute-start.7) | collective-permute-done | bytes 2080 | tf_op jit(solution)/shard_map/ppermute | solution.py:87
  16.9 2.3 %collective-permute-done.6 = f32[4,128]{1,0:T(4,128)S(1)} collective-permute-done((f32[4,128]{1,0:T(4,128)S(1)}, f32[4,128]{1,0:T(4,128)S(1)}, u32[]{:S(2)}, u32[]{:S(2)}) %collective-permute-start.6) | collective-permute-done | bytes 2080 | tf_op jit(solution)/shard_map/ppermute | solution.py:87
  19.2 0.6 %fusion = f32[128]{0:T(128)} fusion(f32[4,128]{1,0:T(4,128)S(1)} %collective-permute-done.8, f32[4,128]{1,0:T(4,128)S(1)} %collective-permute-done.7, f32[4,128]{1,0:T(4,128)S(1)} %collective-permute-done.6, f32[4,128]{1,0:T(4,128)S(1)} %all_results.1, pred[16]{0:T(512)(128)(4,1)S(1)} %and_or_fusion), kind=kLoop, calls=%fused_computation.1 | loop fusion | flops 10112 | bytes 8720 | tf_op jit(solution)/shard_map/reduce_max | solution.py:154
  (2 shorter events, 0.0 us)
Async XLA Ops:
  0.0 3.2 %copy-start.1 = (s32[1,128]{1,0:T(1,128)S(1)}, s32[1,128]{1,0:T(1,128)}, u32[]{:S(2)}) copy-start(s32[1,128]{1,0:T(1,128)} %refs_3_.1) | copy-start | bytes 1540
  0.0 12.4 %collective-permute-start = (bf16[128,768]{1,0:T(8,128)(2,1)}, bf16[128,768]{1,0:T(8,128)(2,1)S(1)}, u32[]{:S(2)}, u32[]{:S(2)}) collective-permute-start(bf16[128,768]{1,0:T(8,128)(2,1)} %bitcast.2), channel_id=1, source_target_pairs={{0,1},{1,0},{2,3},{3,2},{4,5},{5,9},{6,7},{7,11},{8,4},{9,8},{10,6... | collective-permute-start | bytes 589832 | tf_op jit(solution)/shard_map/ppermute | solution.py:87
  0.5 11.9 %collective-permute-start.1 = (bf16[128,768]{1,0:T(8,128)(2,1)}, bf16[128,768]{1,0:T(8,128)(2,1)S(1)}, u32[]{:S(2)}, u32[]{:S(2)}) collective-permute-start(bf16[128,768]{1,0:T(8,128)(2,1)} %bitcast.3), channel_id=1, source_target_pairs={{0,1},{1,9},{2,3},{3,11},{4,0},{5,7},{6,2},{7,5},{8,10},{9,13},{10... | collective-permute-start | bytes 589832 | tf_op jit(solution)/shard_map/ppermute | solution.py:87
  0.6 11.8 %collective-permute-start.2 = (bf16[128,768]{1,0:T(8,128)(2,1)}, bf16[128,768]{1,0:T(8,128)(2,1)S(1)}, u32[]{:S(2)}, u32[]{:S(2)}) collective-permute-start(bf16[128,768]{1,0:T(8,128)(2,1)} %bitcast.4), channel_id=1, source_target_pairs={{0,4},{1,0},{2,6},{3,2},{4,5},{5,1},{6,7},{7,3},{8,12},{9,8},{10,1... | collective-permute-start | bytes 589832 | tf_op jit(solution)/shard_map/ppermute | solution.py:87
  3.2 2.3 %collective-permute-start.3 = (s32[1,128]{1,0:T(1,128)S(1)}, s32[1,128]{1,0:T(1,128)S(1)}, u32[]{:S(2)}, u32[]{:S(2)}) collective-permute-start(s32[1,128]{1,0:T(1,128)S(1)} %copy-done.1), channel_id=1, source_target_pairs={{0,1},{1,0},{2,3},{3,2},{4,5},{5,9},{6,7},{7,11},{8,4},{9,8},{10,6... | collective-permute-start | bytes 1544 | tf_op jit(solution)/shard_map/ppermute | solution.py:87
  4.3 6.8 %collective-permute-start.4 = (s32[1,128]{1,0:T(1,128)S(1)}, s32[1,128]{1,0:T(1,128)S(1)}, u32[]{:S(2)}, u32[]{:S(2)}) collective-permute-start(s32[1,128]{1,0:T(1,128)S(1)} %copy-done.1), channel_id=1, source_target_pairs={{0,1},{1,9},{2,3},{3,11},{4,0},{5,7},{6,2},{7,5},{8,10},{9,13},{10... | collective-permute-start | bytes 1544 | tf_op jit(solution)/shard_map/ppermute | solution.py:87
  4.4 0.9 %copy-start = (bf16[1,128,768]{2,1,0:T(8,128)(2,1)S(1)}, bf16[1,128,768]{2,1,0:T(8,128)(2,1)}, u32[]{:S(2)}) copy-start(bf16[1,128,768]{2,1,0:T(8,128)(2,1)} %param.2) | copy-start | bytes 589828
  5.5 6.9 %collective-permute-start.5 = (s32[1,128]{1,0:T(1,128)S(1)}, s32[1,128]{1,0:T(1,128)S(1)}, u32[]{:S(2)}, u32[]{:S(2)}) collective-permute-start(s32[1,128]{1,0:T(1,128)S(1)} %copy-done.1), channel_id=1, source_target_pairs={{0,4},{1,0},{2,6},{3,2},{4,5},{5,1},{6,7},{7,3},{8,12},{9,8},{10,1... | collective-permute-start | bytes 1544 | tf_op jit(solution)/shard_map/ppermute | solution.py:87
  13.2 2.4 %collective-permute-start.8 = (f32[4,128]{1,0:T(4,128)S(1)}, f32[4,128]{1,0:T(4,128)S(1)}, u32[]{:S(2)}, u32[]{:S(2)}) collective-permute-start(f32[4,128]{1,0:T(4,128)S(1)} %all_results.1), channel_id=1, source_target_pairs={{0,1},{1,0},{2,3},{3,2},{4,8},{5,4},{6,10},{7,6},{8,9},{9,5},{10,1... | collective-permute-start | bytes 6152 | tf_op jit(solution)/shard_map/ppermute | solution.py:87
  13.3 3.6 %collective-permute-start.7 = (f32[4,128]{1,0:T(4,128)S(1)}, f32[4,128]{1,0:T(4,128)S(1)}, u32[]{:S(2)}, u32[]{:S(2)}) collective-permute-start(f32[4,128]{1,0:T(4,128)S(1)} %all_results.1), channel_id=1, source_target_pairs={{0,4},{1,0},{2,6},{3,2},{4,12},{5,7},{6,14},{7,5},{8,9},{9,1},{10,... | collective-permute-start | bytes 6152 | tf_op jit(solution)/shard_map/ppermute | solution.py:87
  15.6 3.6 %collective-permute-start.6 = (f32[4,128]{1,0:T(4,128)S(1)}, f32[4,128]{1,0:T(4,128)S(1)}, u32[]{:S(2)}, u32[]{:S(2)}) collective-permute-start(f32[4,128]{1,0:T(4,128)S(1)} %all_results.1), channel_id=1, source_target_pairs={{0,1},{1,5},{2,3},{3,7},{4,0},{5,4},{6,2},{7,6},{8,9},{9,13},{10,1... | collective-permute-start | bytes 6152 | tf_op jit(solution)/shard_map/ppermute | solution.py:87

commit v2 on v1

--- a/solution.py
+++ b/solution.py
@@ -41,18 +41,19 @@
     return jnp.maximum(nearest, -1.0)[None, :]
 
 
+MEET = ("1o", "2o")
+PLACES = 4
+SWAP = tuple((f"{place}e", f"{place}o") for place in range(PLACES))
 TO_ROOT = (
-    (("2e", "1e", "1o", "2o"), ("0e", "0o"), ("3e", "3o")),
-    (("3e", "1e", "0e", "0o", "2o", "3o"), ("1o~",), ("2e~",)),
-    (("0e", "1e", "1o", "0o"), ("3o", "2o", "2e", "3e")),
+    (("0e", "0o", "2o", "2e", "3o", "3e", "1o", "1e"),),
+    (("0e", "0o"), ("1e~",), ("2e", "1o", "2o"), ("3e", "3o")),
+    (("0e", "1o", "1e", "0o"), ("2e", "3o", "2o"), ("3e~",)),
 )
 BACK = (
-    (("1e", "0e", "0o", "1o"), ("2o", "3o", "3e", "2e")),
-    (("1e", "3e", "2e", "2o", "0o", "0e"), ("1o~",), ("3o~",)),
-    (("1e", "2e", "2o", "1o"), ("0e", "0o"), ("3e", "3o")),
+    (("0e", "2e", "2o", "0o", "1e", "1o"), ("3e", "3o")),
+    (("0e", "0o"), ("1e", "1o", "2e"), ("3e", "2o", "3o")),
+    (("0e", "0o"), ("1e~",), ("2e", "2o", "1o", "3e", "3o")),
 )
-MEET = (1, 2)
-PLACES = 4
 
 
 def following(cycles, spot):
@@ -63,11 +64,11 @@
 
 
 def wanted(place, parity):
-    spot, root = f"{place}{'eo'[parity]}", f"{MEET[parity]}{'eo'[parity]}"
-    if spot == root:
-        return 0
-    block = 1 + [following(cycles, spot) == root for cycles in TO_ROOT].index(True)
-    source = 1 + [following(cycles, root) == spot for cycles in BACK].index(True)
+    spot, root = f"{place}{'eo'[parity]}", MEET[parity]
+    there = [following(cycles, spot) == root for cycles in TO_ROOT]
+    back = [following(cycles, root) == spot for cycles in BACK + (SWAP,)]
+    block = 1 + there.index(True) if True in there else 0
+    source = 1 + back.index(True) if spot != root else 0
     return source * PLACES + block
 
 
@@ -91,16 +92,18 @@
 WHOLE = pl.BlockSpec(memory_space=pltpu.VMEM)
 
 
-def own_body(rows, out):
-    out[...] = normalize(rows[...])
+def first_body(guest, own, other, out):
+    use_other = jnp.max(guest[...], axis=1, keepdims=True) > 0
+    out[...] = normalize(jnp.where(use_other, other[...], own[...]))
 
 
-def root_body(own, *refs):
+def root_body(first, *refs):
     n = PLACES
-    arrived, ids, out = refs[: n - 1], refs[n - 1 : 2 * n - 1], refs[2 * n - 1]
-    count = own.shape[0]
-    normed = jnp.concatenate([own[...]] + [normalize(r[...]) for r in arrived], axis=0)
-    across = jnp.concatenate([i[...] for i in ids], axis=1)
+    arrived, (guest, own_ids, *ids), out = refs[: n - 1], refs[n - 1 : -1], refs[-1]
+    count = first.shape[0]
+    first_ids = jnp.where(guest[...] > 0, ids[-1][...], own_ids[...])
+    normed = jnp.concatenate([first[...]] + [normalize(r[...]) for r in arrived], axis=0)
+    across = jnp.concatenate([first_ids] + [i[...] for i in ids[:-1]], axis=1)
     index = lax.broadcasted_iota(jnp.int32, (1, across.shape[1]), 1)
     down = jnp.transpose(jnp.broadcast_to(across, (8, across.shape[1])))[:, :1]
     down_index = lax.broadcasted_iota(jnp.int32, (down.shape[0], 1), 0)
@@ -111,26 +114,26 @@
         out[k : k + 1, :] = best[:, k * count : (k + 1) * count]
 
 
-def own_rows(rows):
+def first_rows(guest, own, other):
     return pl.pallas_call(
-        own_body,
-        out_shape=jax.ShapeDtypeStruct(rows.shape, jnp.bfloat16),
-        in_specs=[WHOLE],
+        first_body,
+        out_shape=jax.ShapeDtypeStruct(own.shape, jnp.bfloat16),
+        in_specs=[WHOLE] * 3,
         out_specs=WHOLE,
         compiler_params=GRANT,
-        name="own_rows",
-    )(rows)
+        name="first_rows",
+    )(guest, own, other)
 
 
-def all_results(own, arrived, ids):
+def all_results(first, arrived, ids):
     return pl.pallas_call(
         root_body,
-        out_shape=jax.ShapeDtypeStruct((PLACES, own.shape[0]), jnp.float32),
-        in_specs=[WHOLE] * (2 * PLACES),
+        out_shape=jax.ShapeDtypeStruct((PLACES, first.shape[0]), jnp.float32),
+        in_specs=[WHOLE] * (1 + len(arrived) + len(ids)),
         out_specs=WHOLE,
         compiler_params=GRANT,
         name="all_results",
-    )(own, *arrived, *ids)
+    )(first, *arrived, *ids)
 
 
 def at_root(batches):
@@ -139,12 +142,16 @@
 
     def whole(embeddings, cluster_ids):
         rows = embeddings[0]
-        arrived = [travel(rows, cycles, batches) for cycles in TO_ROOT]
-        arrived_ids = [travel(cluster_ids, cycles, batches) for cycles in TO_ROOT]
-        best = all_results(own_rows(rows), arrived, [cluster_ids] + arrived_ids)
-        back = [travel(best, cycles, batches) for cycles in BACK]
+        where_am_i = lax.axis_index(SPAN) * 2 + (lax.axis_index(BATCH) & 1)
+        guest = where_am_i == int(MEET[0][0]) * 2 + "eo".index(MEET[0][1])
+        guest = jnp.broadcast_to(guest.astype(jnp.int32), cluster_ids.shape)
+        inward, outward = TO_ROOT + (SWAP,), BACK + (SWAP,)
+        arrived = [travel(rows, c, batches) for c in inward]
+        arrived_ids = [travel(cluster_ids, c, batches) for c in inward]
+        first = first_rows(guest, rows, arrived[-1])
+        best = all_results(first, arrived[:-1], [guest, cluster_ids] + arrived_ids)
+        back = [travel(best, c, batches) for c in outward]
         stack = jnp.concatenate([best] + back, axis=0)
-        where_am_i = lax.axis_index(SPAN) * 2 + (lax.axis_index(BATCH) & 1)
         row = lax.broadcasted_iota(jnp.int32, stack.shape, 0)
         mine = jnp.zeros(stack.shape, jnp.bool_)
         for place in range(PLACES):

time: 19.9 us -> 20.9 us (1.050)
  waiting for transfers between devices: 4.86 us -> 7.11 us
  starting transfers between devices: 12.4 us -> 10.9 us
    ppermute x9 -> x12, waiting for transfers between devices: 4.86 us -> 7.11 us  [travel(): return lax.ppermute(array, (SPAN, BATCH), pairs(cycles, batches))]
    ppermute x9 -> x12, starting transfers between devices: 12.4 us -> 10.9 us  [travel(): return lax.ppermute(array, (SPAN, BATCH), pairs(cycles, batches))]
  transfers between devices with their start and end apart: 9 -> 12, of which waited for: 3 -> 3; matrix products, arithmetic and copies ran while one was open for 0% -> 0% of each run, Pallas kernels for 1% -> 1%
where the time goes in v2:
time: 20.9 us; the launch traced here: 20.8 us
  starting transfers between devices  10.9 us (52%)
  waiting for transfers between devices  7.11 us (34%)
  Pallas kernels  1.12 us (5%)
  local copies, waits for them, and re-layouts  0.98 us (5%)
  other arithmetic  0.62 us (3%)
    ppermute x12, starting transfers between devices, travel(): return lax.ppermute(array, (SPAN, BATCH), pairs(cycles, batches))  10.9 us
    ppermute x12, waiting for transfers between devices, travel(): return lax.ppermute(array, (SPAN, BATCH), pairs(cycles, batches))  7.11 us
    unnamed x4, local copies, waits for them, and re-layouts  0.93 us
    pallas_call x1, Pallas kernels, all_results(): pl.pallas_call(root_body, out_shape=jax.ShapeDtypeStruct((PLACES, first.s...  0.81 us
    reduce_max x1, other arithmetic, whole(): return jnp.max(jnp.where(mine, stack, -1.0), axis=0)[None, :]  0.6 us
  transfers between devices with their start and end apart: 12, of which 3 were waited for; matrix products, arithmetic and copies ran while one was open for 0% of the time, Pallas kernels for 1%

profile of v2, /device:TPU:0, one launch (start us, length us, event | category | flops | bytes accessed | tf_op | source)
XLA Modules:
  0.0 20.8 jit_solution(14917171564763243846)
XLA Ops:
  0.0 0.5 %collective-permute-start = (bf16[128,768]{1,0:T(8,128)(2,1)}, bf16[128,768]{1,0:T(8,128)(2,1)S(1)}, u32[]{:S(2)}, u32[]{:S(2)}) collective-permute-start(bf16[128,768]{1,0:T(8,128)(2,1)} %bitcast.2), channel_id=1, source_target_pairs={{0,1},{1,0},{2,3},{3,2},{4,5},{5,4},{6,7},{7,6},{8,9},{9,8},{10,11... | collective-permute-start | bytes 589832 | tf_op jit(solution)/shard_map/ppermute | solution.py:88
  0.5 0.1 collective-permute-start.1
  0.6 3.7 %collective-permute-start.2 = (bf16[128,768]{1,0:T(8,128)(2,1)}, bf16[128,768]{1,0:T(8,128)(2,1)S(1)}, u32[]{:S(2)}, u32[]{:S(2)}) collective-permute-start(bf16[128,768]{1,0:T(8,128)(2,1)} %bitcast.4), channel_id=1, source_target_pairs={{0,1},{1,0},{2,3},{3,2},{4,6},{5,9},{6,4},{7,11},{8,5},{9,8},{10,7... | collective-permute-start | bytes 589832 | tf_op jit(solution)/shard_map/ppermute | solution.py:88
  4.3 0.2 %collective-permute-start.3 = (bf16[128,768]{1,0:T(8,128)(2,1)}, bf16[128,768]{1,0:T(8,128)(2,1)S(1)}, u32[]{:S(2)}, u32[]{:S(2)}) collective-permute-start(bf16[128,768]{1,0:T(8,128)(2,1)} %bitcast.5), channel_id=1, source_target_pairs={{0,5},{1,0},{2,7},{3,2},{4,1},{5,4},{6,3},{7,6},{8,13},{9,8},{10,1... | collective-permute-start | bytes 589832 | tf_op jit(solution)/shard_map/ppermute | solution.py:88
  4.5 0.3 %collective-permute-start.4 = (s32[1,128]{1,0:T(1,128)S(1)}, s32[1,128]{1,0:T(1,128)S(1)}, u32[]{:S(2)}, u32[]{:S(2)}) collective-permute-start(s32[1,128]{1,0:T(1,128)S(1)} %copy-done.1), channel_id=1, source_target_pairs={{0,1},{1,9},{2,3},{3,11},{4,0},{5,4},{6,2},{7,6},{8,13},{9,8},{10,... | collective-permute-start | bytes 1544 | tf_op jit(solution)/shard_map/ppermute | solution.py:88
  4.8 5.0 %collective-permute-done.4.refs_5_ = s32[1,128]{1,0:T(1,128)S(1)} collective-permute-done((s32[1,128]{1,0:T(1,128)S(1)}, s32[1,128]{1,0:T(1,128)S(1)}, u32[]{:S(2)}, u32[]{:S(2)}) %collective-permute-start.4) | collective-permute-done | bytes 544 | tf_op jit(solution)/shard_map/ppermute | solution.py:88
  9.8 0.0 collective-permute-start.5
  9.8 1.2 %collective-permute-done.5.refs_6_ = s32[1,128]{1,0:T(1,128)S(1)} collective-permute-done((s32[1,128]{1,0:T(1,128)S(1)}, s32[1,128]{1,0:T(1,128)S(1)}, u32[]{:S(2)}, u32[]{:S(2)}) %collective-permute-start.5) | collective-permute-done | bytes 544 | tf_op jit(solution)/shard_map/ppermute | solution.py:88
  11.0 2.4 %collective-permute-start.6 = (s32[1,128]{1,0:T(1,128)S(1)}, s32[1,128]{1,0:T(1,128)S(1)}, u32[]{:S(2)}, u32[]{:S(2)}) collective-permute-start(s32[1,128]{1,0:T(1,128)S(1)} %copy-done.1), channel_id=1, source_target_pairs={{0,5},{1,0},{2,7},{3,2},{4,1},{5,4},{6,3},{7,6},{8,13},{9,8},{10,1... | collective-permute-start | bytes 1544 | tf_op jit(solution)/shard_map/ppermute | solution.py:88
  13.3 0.0 copy-start
  13.4 0.9 %copy-done = bf16[1,128,768]{2,1,0:T(8,128)(2,1)S(1)} copy-done((bf16[1,128,768]{2,1,0:T(8,128)(2,1)S(1)}, bf16[1,128,768]{2,1,0:T(8,128)(2,1)}, u32[]{:S(2)}) %copy-start) | copy-done | bytes 196632
  14.3 0.3 %first_rows.1.first = bf16[128,768]{1,0:T(8,128)(2,1)S(1)} custom-call(s32[1,128]{1,0:T(1,128)S(1)} %broadcast_in_dim.10.guest.refs_3_, bf16[128,768]{1,0:T(8,128)(2,1)S(1)} %bitcast.6, bf16[128,768]{1,0:T(8,128)(2,1)S(1)} %collective-permute-done.other), custom_call_target="tpu_custom_call" | custom-call | tf_op jit(solution)/shard_map/first_rows/pallas_call | solution.py:118
  14.6 0.0 collective-permute-done.6.refs_7_
  14.6 0.0 collective-permute-done.7.refs_8_
  14.6 0.0 collective-permute-done.1.refs_0_
  14.6 0.0 collective-permute-done.2.refs_1_
  14.7 0.8 %all_results.1 = f32[4,128]{1,0:T(4,128)S(1)} custom-call(bf16[128,768]{1,0:T(8,128)(2,1)S(1)} %first_rows.1.first, bf16[128,768]{1,0:T(8,128)(2,1)S(1)} %collective-permute-done.1.refs_0_, bf16[128,768]{1,0:T(8,128)(2,1)S(1)} %collective-permute-done.2.refs_1_, bf16[128,768]{1,0:T(8,128)(2,1)S(1)} %collective-permute-done.3.refs_2_, ...), custom_call_target="tpu_custom_call" | custom-call | tf_op jit(solution)/shard_map/all_results/pallas_call | solution.py:129
  15.5 0.5 %collective-permute-start.10 = (f32[4,128]{1,0:T(4,128)S(1)}, f32[4,128]{1,0:T(4,128)S(1)}, u32[]{:S(2)}, u32[]{:S(2)}) collective-permute-start(f32[4,128]{1,0:T(4,128)S(1)} %all_results.1), channel_id=1, source_target_pairs={{0,1},{1,0},{2,3},{3,2},{4,6},{5,12},{6,4},{7,14},{8,9},{9,5},{10,... | collective-permute-start | bytes 6152 | tf_op jit(solution)/shard_map/ppermute | solution.py:88
  16.0 0.1 collective-permute-start.11
  16.1 2.7 %collective-permute-start.8 = (f32[4,128]{1,0:T(4,128)S(1)}, f32[4,128]{1,0:T(4,128)S(1)}, u32[]{:S(2)}, u32[]{:S(2)}) collective-permute-start(f32[4,128]{1,0:T(4,128)S(1)} %all_results.1), channel_id=1, source_target_pairs={{0,8},{1,4},{2,10},{3,6},{4,5},{5,0},{6,7},{7,2},{8,9},{9,1},{10,1... | collective-permute-start | bytes 6152 | tf_op jit(solution)/shard_map/ppermute | solution.py:88
  18.8 0.4 %collective-permute-start.9 = (f32[4,128]{1,0:T(4,128)S(1)}, f32[4,128]{1,0:T(4,128)S(1)}, u32[]{:S(2)}, u32[]{:S(2)}) collective-permute-start(f32[4,128]{1,0:T(4,128)S(1)} %all_results.1), channel_id=1, source_target_pairs={{0,1},{1,0},{2,3},{3,2},{4,5},{5,8},{6,7},{7,10},{8,4},{9,13},{10,... | collective-permute-start | bytes 6152 | tf_op jit(solution)/shard_map/ppermute | solution.py:88
  19.2 0.9 %collective-permute-done.8 = f32[4,128]{1,0:T(4,128)S(1)} collective-permute-done((f32[4,128]{1,0:T(4,128)S(1)}, f32[4,128]{1,0:T(4,128)S(1)}, u32[]{:S(2)}, u32[]{:S(2)}) %collective-permute-start.8) | collective-permute-done | bytes 2080 | tf_op jit(solution)/shard_map/ppermute | solution.py:88
  20.1 0.1 concatenate.3
  20.2 0.6 %select_reduce_fusion = f32[128]{0:T(128)} fusion(f32[20,128]{1,0:T(8,128)S(1)} %concatenate.3, pred[20]{0:T(512)(128)(4,1)S(1)} %and_or_fusion), kind=kLoop, calls=%fused_computation | loop fusion | flops 4992 | bytes 10772 | tf_op jit(solution)/shard_map/reduce_max | solution.py:161
  (10 shorter events, 0.0 us)
Async XLA Ops:
  0.0 4.5 %copy-start.1 = (s32[1,128]{1,0:T(1,128)S(1)}, s32[1,128]{1,0:T(1,128)}, u32[]{:S(2)}) copy-start(s32[1,128]{1,0:T(1,128)} %refs_4_.1) | copy-start | bytes 1540
  0.0 13.3 %collective-permute-start = (bf16[128,768]{1,0:T(8,128)(2,1)}, bf16[128,768]{1,0:T(8,128)(2,1)S(1)}, u32[]{:S(2)}, u32[]{:S(2)}) collective-permute-start(bf16[128,768]{1,0:T(8,128)(2,1)} %bitcast.2), channel_id=1, source_target_pairs={{0,1},{1,0},{2,3},{3,2},{4,5},{5,4},{6,7},{7,6},{8,9},{9,8},{10,11... | collective-permute-start | bytes 589832 | tf_op jit(solution)/shard_map/ppermute | solution.py:88
  0.5 14.1 %collective-permute-start.1 = (bf16[128,768]{1,0:T(8,128)(2,1)}, bf16[128,768]{1,0:T(8,128)(2,1)S(1)}, u32[]{:S(2)}, u32[]{:S(2)}) collective-permute-start(bf16[128,768]{1,0:T(8,128)(2,1)} %bitcast.3), channel_id=1, source_target_pairs={{0,1},{1,9},{2,3},{3,11},{4,0},{5,4},{6,2},{7,6},{8,13},{9,8},{10,... | collective-permute-start | bytes 589832 | tf_op jit(solution)/shard_map/ppermute | solution.py:88
  0.6 14.1 %collective-permute-start.2 = (bf16[128,768]{1,0:T(8,128)(2,1)}, bf16[128,768]{1,0:T(8,128)(2,1)S(1)}, u32[]{:S(2)}, u32[]{:S(2)}) collective-permute-start(bf16[128,768]{1,0:T(8,128)(2,1)} %bitcast.4), channel_id=1, source_target_pairs={{0,1},{1,0},{2,3},{3,2},{4,6},{5,9},{6,4},{7,11},{8,5},{9,8},{10,7... | collective-permute-start | bytes 589832 | tf_op jit(solution)/shard_map/ppermute | solution.py:88
  4.3 10.3 %collective-permute-start.3 = (bf16[128,768]{1,0:T(8,128)(2,1)}, bf16[128,768]{1,0:T(8,128)(2,1)S(1)}, u32[]{:S(2)}, u32[]{:S(2)}) collective-permute-start(bf16[128,768]{1,0:T(8,128)(2,1)} %bitcast.5), channel_id=1, source_target_pairs={{0,5},{1,0},{2,7},{3,2},{4,1},{5,4},{6,3},{7,6},{8,13},{9,8},{10,1... | collective-permute-start | bytes 589832 | tf_op jit(solution)/shard_map/ppermute | solution.py:88
  4.5 5.3 %collective-permute-start.4 = (s32[1,128]{1,0:T(1,128)S(1)}, s32[1,128]{1,0:T(1,128)S(1)}, u32[]{:S(2)}, u32[]{:S(2)}) collective-permute-start(s32[1,128]{1,0:T(1,128)S(1)} %copy-done.1), channel_id=1, source_target_pairs={{0,1},{1,9},{2,3},{3,11},{4,0},{5,4},{6,2},{7,6},{8,13},{9,8},{10,... | collective-permute-start | bytes 1544 | tf_op jit(solution)/shard_map/ppermute | solution.py:88
  9.8 1.2 %collective-permute-start.5 = (s32[1,128]{1,0:T(1,128)S(1)}, s32[1,128]{1,0:T(1,128)S(1)}, u32[]{:S(2)}, u32[]{:S(2)}) collective-permute-start(s32[1,128]{1,0:T(1,128)S(1)} %copy-done.1), channel_id=1, source_target_pairs={{0,1},{1,0},{2,3},{3,2},{4,6},{5,9},{6,4},{7,11},{8,5},{9,8},{10,7... | collective-permute-start | bytes 1544 | tf_op jit(solution)/shard_map/ppermute | solution.py:88
  11.0 3.7 %collective-permute-start.6 = (s32[1,128]{1,0:T(1,128)S(1)}, s32[1,128]{1,0:T(1,128)S(1)}, u32[]{:S(2)}, u32[]{:S(2)}) collective-permute-start(s32[1,128]{1,0:T(1,128)S(1)} %copy-done.1), channel_id=1, source_target_pairs={{0,5},{1,0},{2,7},{3,2},{4,1},{5,4},{6,3},{7,6},{8,13},{9,8},{10,1... | collective-permute-start | bytes 1544 | tf_op jit(solution)/shard_map/ppermute | solution.py:88
  13.3 1.3 %collective-permute-start.7 = (s32[1,128]{1,0:T(1,128)S(1)}, s32[1,128]{1,0:T(1,128)S(1)}, u32[]{:S(2)}, u32[]{:S(2)}) collective-permute-start(s32[1,128]{1,0:T(1,128)S(1)} %copy-done.1), channel_id=1, source_target_pairs={{0,1},{1,0},{2,3},{3,2},{4,5},{5,4},{6,7},{7,6},{8,9},{9,8},{10,11... | collective-permute-start | bytes 1544 | tf_op jit(solution)/shard_map/ppermute | solution.py:88
  13.3 0.9 %copy-start = (bf16[1,128,768]{2,1,0:T(8,128)(2,1)S(1)}, bf16[1,128,768]{2,1,0:T(8,128)(2,1)}, u32[]{:S(2)}) copy-start(bf16[1,128,768]{2,1,0:T(8,128)(2,1)} %param.2) | copy-start | bytes 589828
  15.5 3.7 %collective-permute-start.10 = (f32[4,128]{1,0:T(4,128)S(1)}, f32[4,128]{1,0:T(4,128)S(1)}, u32[]{:S(2)}, u32[]{:S(2)}) collective-permute-start(f32[4,128]{1,0:T(4,128)S(1)} %all_results.1), channel_id=1, source_target_pairs={{0,1},{1,0},{2,3},{3,2},{4,6},{5,12},{6,4},{7,14},{8,9},{9,5},{10,... | collective-permute-start | bytes 6152 | tf_op jit(solution)/shard_map/ppermute | solution.py:88
  16.0 3.2 %collective-permute-start.11 = (f32[4,128]{1,0:T(4,128)S(1)}, f32[4,128]{1,0:T(4,128)S(1)}, u32[]{:S(2)}, u32[]{:S(2)}) collective-permute-start(f32[4,128]{1,0:T(4,128)S(1)} %all_results.1), channel_id=1, source_target_pairs={{0,1},{1,0},{2,3},{3,2},{4,5},{5,4},{6,7},{7,6},{8,9},{9,8},{10,11... | collective-permute-start | bytes 6152 | tf_op jit(solution)/shard_map/ppermute | solution.py:88
  16.1 4.0 %collective-permute-start.8 = (f32[4,128]{1,0:T(4,128)S(1)}, f32[4,128]{1,0:T(4,128)S(1)}, u32[]{:S(2)}, u32[]{:S(2)}) collective-permute-start(f32[4,128]{1,0:T(4,128)S(1)} %all_results.1), channel_id=1, source_target_pairs={{0,8},{1,4},{2,10},{3,6},{4,5},{5,0},{6,7},{7,2},{8,9},{9,1},{10,1... | collective-permute-start | bytes 6152 | tf_op jit(solution)/shard_map/ppermute | solution.py:88
  18.8 1.3 %collective-permute-start.9 = (f32[4,128]{1,0:T(4,128)S(1)}, f32[4,128]{1,0:T(4,128)S(1)}, u32[]{:S(2)}, u32[]{:S(2)}) collective-permute-start(f32[4,128]{1,0:T(4,128)S(1)} %all_results.1), channel_id=1, source_target_pairs={{0,1},{1,0},{2,3},{3,2},{4,5},{5,8},{6,7},{7,10},{8,4},{9,13},{10,... | collective-permute-start | bytes 6152 | tf_op jit(solution)/shard_map/ppermute | solution.py:88

commit v3 on v2

--- a/solution.py
+++ b/solution.py
@@ -92,48 +92,85 @@
 WHOLE = pl.BlockSpec(memory_space=pltpu.VMEM)
 
 
-def first_body(guest, own, other, out):
+def column_of(row):
+    return jnp.transpose(jnp.broadcast_to(row, (8, row.shape[1])))[:, :1]
+
+
+def best_of(scores, keep):
+    return jnp.max(jnp.where(keep, scores, -1.0), axis=0, keepdims=True)
+
+
+def own_body(rows, out):
+    out[...] = normalize(rows[...])
+
+
+def early_body(guest, own, other, raw, normed, scores):
+    count = own.shape[0]
     use_other = jnp.max(guest[...], axis=1, keepdims=True) > 0
-    out[...] = normalize(jnp.where(use_other, other[...], own[...]))
-
-
-def root_body(first, *refs):
-    n = PLACES
-    arrived, (guest, own_ids, *ids), out = refs[: n - 1], refs[n - 1 : -1], refs[-1]
-    count = first.shape[0]
-    first_ids = jnp.where(guest[...] > 0, ids[-1][...], own_ids[...])
-    normed = jnp.concatenate([first[...]] + [normalize(r[...]) for r in arrived], axis=0)
-    across = jnp.concatenate([first_ids] + [i[...] for i in ids[:-1]], axis=1)
-    index = lax.broadcasted_iota(jnp.int32, (1, across.shape[1]), 1)
-    down = jnp.transpose(jnp.broadcast_to(across, (8, across.shape[1])))[:, :1]
-    down_index = lax.broadcasted_iota(jnp.int32, (down.shape[0], 1), 0)
-    scores = pair_scores(normed, normed)
-    keep = (down == across) & (down_index != index)
-    best = jnp.maximum(jnp.max(jnp.where(keep, scores, -1.0), axis=0, keepdims=True), -1.0)
-    for k in range(n):
-        out[k : k + 1, :] = best[:, k * count : (k + 1) * count]
-
-
-def first_rows(guest, own, other):
+    normed[:count, :] = jnp.where(use_other, normalize(other[...]), own[...])
+    normed[count:, :] = normalize(raw[...])
+    scores[...] = pair_scores(normed[...], normed[...])
+
+
+def late_body(normed, scores, guest, own_ids, other_ids, early_id, id1, id2, raw1, raw2, out):
+    count, half = raw1.shape[0], normed.shape[0]
+    first = jnp.where(guest[...] > 0, other_ids[...], own_ids[...])
+    early_row = jnp.concatenate([first, early_id[...]], axis=1)
+    late_row = jnp.concatenate([id1[...], id2[...]], axis=1)
+    early_column, late_column = column_of(early_row), column_of(late_row)
+    below = lax.broadcasted_iota(jnp.int32, (half, half), 0)
+    beside = lax.broadcasted_iota(jnp.int32, (half, half), 1)
+    apart = below != beside
+    late = jnp.concatenate([normalize(raw1[...]), normalize(raw2[...])], axis=0)
+    cross = pair_scores(normed[...], late)
+    cross = jnp.where(early_column == late_row, cross, -1.0)
+    inner = best_of(pair_scores(late, late), (late_column == late_row) & apart)
+    late_best = jnp.maximum(jnp.max(cross, axis=0, keepdims=True), inner)
+    across = jnp.maximum(cross[:, :count], cross[:, count:])
+    across = jnp.max(jnp.transpose(across), axis=0, keepdims=True)
+    early_best = best_of(scores[...], (early_column == early_row) & apart)
+    early_best = jnp.maximum(early_best, across)
+    for k, best in enumerate((early_best, late_best)):
+        best = jnp.maximum(best, -1.0)
+        out[2 * k : 2 * k + 1, :] = best[:, :count]
+        out[2 * k + 1 : 2 * k + 2, :] = best[:, count:]
+
+
+def own_rows(rows):
     return pl.pallas_call(
-        first_body,
-        out_shape=jax.ShapeDtypeStruct(own.shape, jnp.bfloat16),
-        in_specs=[WHOLE] * 3,
+        own_body,
+        out_shape=jax.ShapeDtypeStruct(rows.shape, rows.dtype),
+        in_specs=[WHOLE],
         out_specs=WHOLE,
         compiler_params=GRANT,
-        name="first_rows",
-    )(guest, own, other)
-
-
-def all_results(first, arrived, ids):
+        name="own_rows",
+    )(rows)
+
+
+def early_pairs(guest, own, other, raw):
+    rows, width = 2 * own.shape[0], own.shape[1]
     return pl.pallas_call(
-        root_body,
-        out_shape=jax.ShapeDtypeStruct((PLACES, first.shape[0]), jnp.float32),
-        in_specs=[WHOLE] * (1 + len(arrived) + len(ids)),
+        early_body,
+        out_shape=(
+            jax.ShapeDtypeStruct((rows, width), jnp.bfloat16),
+            jax.ShapeDtypeStruct((rows, rows), jnp.float32),
+        ),
+        in_specs=[WHOLE] * 4,
+        out_specs=(WHOLE, WHOLE),
+        compiler_params=GRANT,
+        name="early_pairs",
+    )(guest, own, other, raw)
+
+
+def all_results(*args):
+    return pl.pallas_call(
+        late_body,
+        out_shape=jax.ShapeDtypeStruct((PLACES, args[-1].shape[0]), jnp.float32),
+        in_specs=[WHOLE] * len(args),
         out_specs=WHOLE,
         compiler_params=GRANT,
         name="all_results",
-    )(first, *arrived, *ids)
+    )(*args)
 
 
 def at_root(batches):
@@ -148,8 +185,9 @@
         inward, outward = TO_ROOT + (SWAP,), BACK + (SWAP,)
         arrived = [travel(rows, c, batches) for c in inward]
         arrived_ids = [travel(cluster_ids, c, batches) for c in inward]
-        first = first_rows(guest, rows, arrived[-1])
-        best = all_results(first, arrived[:-1], [guest, cluster_ids] + arrived_ids)
+        normed, scores = early_pairs(guest, own_rows(rows), arrived[-1], arrived[0])
+        ids = [guest, cluster_ids, arrived_ids[-1]] + arrived_ids[:-1]
+        best = all_results(normed, scores, *ids, *arrived[1:-1])
         back = [travel(best, c, batches) for c in outward]
         stack = jnp.concatenate([best] + back, axis=0)
         row = lax.broadcasted_iota(jnp.int32, stack.shape, 0)

time: 20.9 us -> 17.6 us (0.84)
  waiting for transfers between devices: 7.11 us -> 2.15 us
  starting transfers between devices: 10.9 us -> 12.4 us
    ppermute x12, waiting for transfers between devices: 7.11 us -> 2.15 us  [travel(): return lax.ppermute(array, (SPAN, BATCH), pairs(cycles, batches))]
    ppermute x12, starting transfers between devices: 10.9 us -> 12.4 us  [travel(): return lax.ppermute(array, (SPAN, BATCH), pairs(cycles, batches))]
    pallas_call x2 -> x3, Pallas kernels: 1.12 us -> 1.21 us  [the longest x1 0.61 us: all_results(): pl.pallas_call(late_body, out_shape=jax.ShapeDtypeStruct((PLACES, args[-1...]
  transfers between devices with their start and end apart: 12 -> 12, of which waited for: 3 -> 3; matrix products, arithmetic and copies ran while one was open for 0% -> 0% of each run, Pallas kernels for 1% -> 3%
where the time goes in v3:
time: 17.6 us; the launch traced here: 17.5 us
  starting transfers between devices  12.4 us (70%)
  waiting for transfers between devices  2.15 us (12%)
  Pallas kernels  1.21 us (7%)
  local copies, waits for them, and re-layouts  0.98 us (6%)
  other arithmetic  0.62 us (4%)
    ppermute x12, starting transfers between devices, travel(): return lax.ppermute(array, (SPAN, BATCH), pairs(cycles, batches))  12.4 us
    ppermute x12, waiting for transfers between devices, travel(): return lax.ppermute(array, (SPAN, BATCH), pairs(cycles, batches))  2.15 us
    unnamed x4, local copies, waits for them, and re-layouts  0.93 us
    pallas_call x1, Pallas kernels, all_results(): pl.pallas_call(late_body, out_shape=jax.ShapeDtypeStruct((PLACES, args[-1...  0.61 us
    reduce_max x1, other arithmetic, whole(): return jnp.max(jnp.where(mine, stack, -1.0), axis=0)[None, :]  0.6 us
    pallas_call x1, Pallas kernels, early_pairs(): pl.pallas_call(early_body, out_shape=(jax.ShapeDtypeStruct((rows, width),...  0.47 us
  transfers between devices with their start and end apart: 12, of which 3 were waited for; matrix products, arithmetic and copies ran while one was open for 0% of the time, Pallas kernels for 3%

profile of v3, /device:TPU:0, one launch (start us, length us, event | category | flops | bytes accessed | tf_op | source)
XLA Modules:
  0.0 17.5 jit_solution(15203285674636239467)
XLA Ops:
  0.0 0.5 %collective-permute-start = (bf16[128,768]{1,0:T(8,128)(2,1)}, bf16[128,768]{1,0:T(8,128)(2,1)S(1)}, u32[]{:S(2)}, u32[]{:S(2)}) collective-permute-start(bf16[128,768]{1,0:T(8,128)(2,1)} %bitcast.2), channel_id=1, source_target_pairs={{0,1},{1,0},{2,3},{3,2},{4,5},{5,4},{6,7},{7,6},{8,9},{9,8},{10,11... | collective-permute-start | bytes 589832 | tf_op jit(solution)/shard_map/ppermute | solution.py:88
  0.5 0.1 collective-permute-start.1
  0.6 3.7 %collective-permute-start.6 = (bf16[128,768]{1,0:T(8,128)(2,1)}, bf16[128,768]{1,0:T(8,128)(2,1)S(1)}, u32[]{:S(2)}, u32[]{:S(2)}) collective-permute-start(bf16[128,768]{1,0:T(8,128)(2,1)} %bitcast.4), channel_id=1, source_target_pairs={{0,1},{1,0},{2,3},{3,2},{4,6},{5,9},{6,4},{7,11},{8,5},{9,8},{10,7... | collective-permute-start | bytes 589832 | tf_op jit(solution)/shard_map/ppermute | solution.py:88
  4.3 0.2 %collective-permute-start.7 = (bf16[128,768]{1,0:T(8,128)(2,1)}, bf16[128,768]{1,0:T(8,128)(2,1)S(1)}, u32[]{:S(2)}, u32[]{:S(2)}) collective-permute-start(bf16[128,768]{1,0:T(8,128)(2,1)} %bitcast.5), channel_id=1, source_target_pairs={{0,5},{1,0},{2,7},{3,2},{4,1},{5,4},{6,3},{7,6},{8,13},{9,8},{10,1... | collective-permute-start | bytes 589832 | tf_op jit(solution)/shard_map/ppermute | solution.py:88
  4.5 0.3 %collective-permute-start.2 = (s32[1,128]{1,0:T(1,128)S(1)}, s32[1,128]{1,0:T(1,128)S(1)}, u32[]{:S(2)}, u32[]{:S(2)}) collective-permute-start(s32[1,128]{1,0:T(1,128)S(1)} %copy-done.1), channel_id=1, source_target_pairs={{0,1},{1,0},{2,3},{3,2},{4,5},{5,4},{6,7},{7,6},{8,9},{9,8},{10,11... | collective-permute-start | bytes 1544 | tf_op jit(solution)/shard_map/ppermute | solution.py:88
  4.8 0.9 %copy-done = bf16[1,128,768]{2,1,0:T(8,128)(2,1)S(1)} copy-done((bf16[1,128,768]{2,1,0:T(8,128)(2,1)S(1)}, bf16[1,128,768]{2,1,0:T(8,128)(2,1)}, u32[]{:S(2)}) %copy-start) | copy-done | bytes 196632
  5.7 0.1 own_rows.1.own
  5.9 0.1 collective-permute-done.2.other_ids
  6.0 0.2 %collective-permute-start.3 = (s32[1,128]{1,0:T(1,128)S(1)}, s32[1,128]{1,0:T(1,128)S(1)}, u32[]{:S(2)}, u32[]{:S(2)}) collective-permute-start(s32[1,128]{1,0:T(1,128)S(1)} %copy-done.1), channel_id=1, source_target_pairs={{0,1},{1,9},{2,3},{3,11},{4,0},{5,4},{6,2},{7,6},{8,13},{9,8},{10,... | collective-permute-start | bytes 1544 | tf_op jit(solution)/shard_map/ppermute | solution.py:88
  6.2 0.0 collective-permute-done.other
  6.2 1.4 %collective-permute-start.4 = (s32[1,128]{1,0:T(1,128)S(1)}, s32[1,128]{1,0:T(1,128)S(1)}, u32[]{:S(2)}, u32[]{:S(2)}) collective-permute-start(s32[1,128]{1,0:T(1,128)S(1)} %copy-done.1), channel_id=1, source_target_pairs={{0,1},{1,0},{2,3},{3,2},{4,6},{5,9},{6,4},{7,11},{8,5},{9,8},{10,7... | collective-permute-start | bytes 1544 | tf_op jit(solution)/shard_map/ppermute | solution.py:88
  7.6 0.0 collective-permute-done.1.raw
  7.6 2.6 %collective-permute-start.5 = (s32[1,128]{1,0:T(1,128)S(1)}, s32[1,128]{1,0:T(1,128)S(1)}, u32[]{:S(2)}, u32[]{:S(2)}) collective-permute-start(s32[1,128]{1,0:T(1,128)S(1)} %copy-done.1), channel_id=1, source_target_pairs={{0,5},{1,0},{2,7},{3,2},{4,1},{5,4},{6,3},{7,6},{8,13},{9,8},{10,1... | collective-permute-start | bytes 1544 | tf_op jit(solution)/shard_map/ppermute | solution.py:88
  10.2 0.5 %early_pairs.1 = (bf16[256,768]{1,0:T(8,128)(2,1)S(1)}, f32[256,256]{1,0:T(8,128)S(1)}) custom-call(s32[1,128]{1,0:T(1,128)S(1)} %broadcast_in_dim.10.guest, bf16[128,768]{1,0:T(8,128)(2,1)S(1)} %own_rows.1.own, bf16[128,768]{1,0:T(8,128)(2,1)S(1)} %collective-permute-done.other, bf16[128,768]{1,0:T(8,128)(2,1)S(1)} %collective-permute-done.1.raw), custom_call_target="tpu_custom_call" | custom-call | tf_op jit(solution)/shard_map/early_pairs/pallas_call | solution.py:152
  10.7 0.0 collective-permute-done.3.early_id
  10.7 0.0 collective-permute-done.4.id1
  10.7 0.8 %collective-permute-done.5.id2 = s32[1,128]{1,0:T(1,128)S(1)} collective-permute-done((s32[1,128]{1,0:T(1,128)S(1)}, s32[1,128]{1,0:T(1,128)S(1)}, u32[]{:S(2)}, u32[]{:S(2)}) %collective-permute-start.5) | collective-permute-done | bytes 544 | tf_op jit(solution)/shard_map/ppermute | solution.py:88
  11.6 0.6 %all_results.1 = f32[4,128]{1,0:T(4,128)S(1)} custom-call(bf16[256,768]{1,0:T(8,128)(2,1)S(1)} %get-tuple-element.7.normed, f32[256,256]{1,0:T(8,128)S(1)} %get-tuple-element.8.scores, s32[1,128]{1,0:T(1,128)S(1)} %broadcast_in_dim.10.guest, s32[1,128]{1,0:T(1,128)S(1)} %copy-done.1, s32[1,128]{1,0:T(1,128)S(1)} %collective-permute-done.2.other_ids, ...), custom_call_target="tpu_custom_call" | custom-call | tf_op jit(solution)/shard_map/all_results/pallas_call | solution.py:166
  12.2 0.1 collective-permute-start.10
  12.2 0.5 %collective-permute-start.11 = (f32[4,128]{1,0:T(4,128)S(1)}, f32[4,128]{1,0:T(4,128)S(1)}, u32[]{:S(2)}, u32[]{:S(2)}) collective-permute-start(f32[4,128]{1,0:T(4,128)S(1)} %all_results.1), channel_id=1, source_target_pairs={{0,1},{1,0},{2,3},{3,2},{4,5},{5,4},{6,7},{7,6},{8,9},{9,8},{10,11... | collective-permute-start | bytes 6152 | tf_op jit(solution)/shard_map/ppermute | solution.py:88
  12.7 2.8 %collective-permute-start.8 = (f32[4,128]{1,0:T(4,128)S(1)}, f32[4,128]{1,0:T(4,128)S(1)}, u32[]{:S(2)}, u32[]{:S(2)}) collective-permute-start(f32[4,128]{1,0:T(4,128)S(1)} %all_results.1), channel_id=1, source_target_pairs={{0,8},{1,4},{2,10},{3,6},{4,5},{5,0},{6,7},{7,2},{8,9},{9,1},{10,1... | collective-permute-start | bytes 6152 | tf_op jit(solution)/shard_map/ppermute | solution.py:88
  15.5 1.3 %collective-permute-done.8 = f32[4,128]{1,0:T(4,128)S(1)} collective-permute-done((f32[4,128]{1,0:T(4,128)S(1)}, f32[4,128]{1,0:T(4,128)S(1)}, u32[]{:S(2)}, u32[]{:S(2)}) %collective-permute-start.8) | collective-permute-done | bytes 2080 | tf_op jit(solution)/shard_map/ppermute | solution.py:88
  16.8 0.1 concatenate.3
  16.9 0.6 %select_reduce_fusion = f32[128]{0:T(128)} fusion(f32[20,128]{1,0:T(8,128)S(1)} %concatenate.3, pred[20]{0:T(512)(128)(4,1)S(1)} %and_or_fusion), kind=kLoop, calls=%fused_computation | loop fusion | flops 4992 | bytes 10772 | tf_op jit(solution)/shard_map/reduce_max | solution.py:199
  (11 shorter events, 0.0 us)
Async XLA Ops:
  0.0 4.5 %copy-start.1 = (s32[1,128]{1,0:T(1,128)S(1)}, s32[1,128]{1,0:T(1,128)}, u32[]{:S(2)}) copy-start(s32[1,128]{1,0:T(1,128)} %own_ids.1) | copy-start | bytes 1540
  0.0 6.2 %collective-permute-start = (bf16[128,768]{1,0:T(8,128)(2,1)}, bf16[128,768]{1,0:T(8,128)(2,1)S(1)}, u32[]{:S(2)}, u32[]{:S(2)}) collective-permute-start(bf16[128,768]{1,0:T(8,128)(2,1)} %bitcast.2), channel_id=1, source_target_pairs={{0,1},{1,0},{2,3},{3,2},{4,5},{5,4},{6,7},{7,6},{8,9},{9,8},{10,11... | collective-permute-start | bytes 589832 | tf_op jit(solution)/shard_map/ppermute | solution.py:88
  0.5 7.1 %collective-permute-start.1 = (bf16[128,768]{1,0:T(8,128)(2,1)}, bf16[128,768]{1,0:T(8,128)(2,1)S(1)}, u32[]{:S(2)}, u32[]{:S(2)}) collective-permute-start(bf16[128,768]{1,0:T(8,128)(2,1)} %bitcast.3), channel_id=1, source_target_pairs={{0,1},{1,9},{2,3},{3,11},{4,0},{5,4},{6,2},{7,6},{8,13},{9,8},{10,... | collective-permute-start | bytes 589832 | tf_op jit(solution)/shard_map/ppermute | solution.py:88
  0.6 11.0 %collective-permute-start.6 = (bf16[128,768]{1,0:T(8,128)(2,1)}, bf16[128,768]{1,0:T(8,128)(2,1)S(1)}, u32[]{:S(2)}, u32[]{:S(2)}) collective-permute-start(bf16[128,768]{1,0:T(8,128)(2,1)} %bitcast.4), channel_id=1, source_target_pairs={{0,1},{1,0},{2,3},{3,2},{4,6},{5,9},{6,4},{7,11},{8,5},{9,8},{10,7... | collective-permute-start | bytes 589832 | tf_op jit(solution)/shard_map/ppermute | solution.py:88
  4.3 7.3 %collective-permute-start.7 = (bf16[128,768]{1,0:T(8,128)(2,1)}, bf16[128,768]{1,0:T(8,128)(2,1)S(1)}, u32[]{:S(2)}, u32[]{:S(2)}) collective-permute-start(bf16[128,768]{1,0:T(8,128)(2,1)} %bitcast.5), channel_id=1, source_target_pairs={{0,5},{1,0},{2,7},{3,2},{4,1},{5,4},{6,3},{7,6},{8,13},{9,8},{10,1... | collective-permute-start | bytes 589832 | tf_op jit(solution)/shard_map/ppermute | solution.py:88
  4.5 1.4 %collective-permute-start.2 = (s32[1,128]{1,0:T(1,128)S(1)}, s32[1,128]{1,0:T(1,128)S(1)}, u32[]{:S(2)}, u32[]{:S(2)}) collective-permute-start(s32[1,128]{1,0:T(1,128)S(1)} %copy-done.1), channel_id=1, source_target_pairs={{0,1},{1,0},{2,3},{3,2},{4,5},{5,4},{6,7},{7,6},{8,9},{9,8},{10,11... | collective-permute-start | bytes 1544 | tf_op jit(solution)/shard_map/ppermute | solution.py:88
  4.8 0.9 %copy-start = (bf16[1,128,768]{2,1,0:T(8,128)(2,1)S(1)}, bf16[1,128,768]{2,1,0:T(8,128)(2,1)}, u32[]{:S(2)}) copy-start(bf16[1,128,768]{2,1,0:T(8,128)(2,1)} %param.2) | copy-start | bytes 589828
  6.0 4.8 %collective-permute-start.3 = (s32[1,128]{1,0:T(1,128)S(1)}, s32[1,128]{1,0:T(1,128)S(1)}, u32[]{:S(2)}, u32[]{:S(2)}) collective-permute-start(s32[1,128]{1,0:T(1,128)S(1)} %copy-done.1), channel_id=1, source_target_pairs={{0,1},{1,9},{2,3},{3,11},{4,0},{5,4},{6,2},{7,6},{8,13},{9,8},{10,... | collective-permute-start | bytes 1544 | tf_op jit(solution)/shard_map/ppermute | solution.py:88
  6.2 4.5 %collective-permute-start.4 = (s32[1,128]{1,0:T(1,128)S(1)}, s32[1,128]{1,0:T(1,128)S(1)}, u32[]{:S(2)}, u32[]{:S(2)}) collective-permute-start(s32[1,128]{1,0:T(1,128)S(1)} %copy-done.1), channel_id=1, source_target_pairs={{0,1},{1,0},{2,3},{3,2},{4,6},{5,9},{6,4},{7,11},{8,5},{9,8},{10,7... | collective-permute-start | bytes 1544 | tf_op jit(solution)/shard_map/ppermute | solution.py:88
  7.6 3.9 %collective-permute-start.5 = (s32[1,128]{1,0:T(1,128)S(1)}, s32[1,128]{1,0:T(1,128)S(1)}, u32[]{:S(2)}, u32[]{:S(2)}) collective-permute-start(s32[1,128]{1,0:T(1,128)S(1)} %copy-done.1), channel_id=1, source_target_pairs={{0,5},{1,0},{2,7},{3,2},{4,1},{5,4},{6,3},{7,6},{8,13},{9,8},{10,1... | collective-permute-start | bytes 1544 | tf_op jit(solution)/shard_map/ppermute | solution.py:88
  12.2 3.4 %collective-permute-start.10 = (f32[4,128]{1,0:T(4,128)S(1)}, f32[4,128]{1,0:T(4,128)S(1)}, u32[]{:S(2)}, u32[]{:S(2)}) collective-permute-start(f32[4,128]{1,0:T(4,128)S(1)} %all_results.1), channel_id=1, source_target_pairs={{0,1},{1,0},{2,3},{3,2},{4,6},{5,12},{6,4},{7,14},{8,9},{9,5},{10,... | collective-permute-start | bytes 6152 | tf_op jit(solution)/shard_map/ppermute | solution.py:88
  12.2 3.3 %collective-permute-start.11 = (f32[4,128]{1,0:T(4,128)S(1)}, f32[4,128]{1,0:T(4,128)S(1)}, u32[]{:S(2)}, u32[]{:S(2)}) collective-permute-start(f32[4,128]{1,0:T(4,128)S(1)} %all_results.1), channel_id=1, source_target_pairs={{0,1},{1,0},{2,3},{3,2},{4,5},{5,4},{6,7},{7,6},{8,9},{9,8},{10,11... | collective-permute-start | bytes 6152 | tf_op jit(solution)/shard_map/ppermute | solution.py:88
  12.7 4.1 %collective-permute-start.8 = (f32[4,128]{1,0:T(4,128)S(1)}, f32[4,128]{1,0:T(4,128)S(1)}, u32[]{:S(2)}, u32[]{:S(2)}) collective-permute-start(f32[4,128]{1,0:T(4,128)S(1)} %all_results.1), channel_id=1, source_target_pairs={{0,8},{1,4},{2,10},{3,6},{4,5},{5,0},{6,7},{7,2},{8,9},{9,1},{10,1... | collective-permute-start | bytes 6152 | tf_op jit(solution)/shard_map/ppermute | solution.py:88
  15.5 1.3 %collective-permute-start.9 = (f32[4,128]{1,0:T(4,128)S(1)}, f32[4,128]{1,0:T(4,128)S(1)}, u32[]{:S(2)}, u32[]{:S(2)}) collective-permute-start(f32[4,128]{1,0:T(4,128)S(1)} %all_results.1), channel_id=1, source_target_pairs={{0,1},{1,0},{2,3},{3,2},{4,5},{5,8},{6,7},{7,10},{8,4},{9,13},{10,... | collective-permute-start | bytes 6152 | tf_op jit(solution)/shard_map/ppermute | solution.py:88

commit v4 on v3

--- a/solution.py
+++ b/solution.py
@@ -52,7 +52,7 @@
 BACK = (
     (("0e", "2e", "2o", "0o", "1e", "1o"), ("3e", "3o")),
     (("0e", "0o"), ("1e", "1o", "2e"), ("3e", "2o", "3o")),
-    (("0e", "0o"), ("1e~",), ("2e", "2o", "1o", "3e", "3o")),
+    (("0e", "0o"), ("1e", "2o", "1o", "3e", "3o", "2e")),
 )
 
 
@@ -63,13 +63,20 @@
             return names[(names.index(spot) + 1) % len(names)]
 
 
-def wanted(place, parity):
-    spot, root = f"{place}{'eo'[parity]}", MEET[parity]
-    there = [following(cycles, spot) == root for cycles in TO_ROOT]
+def block_of(spot):
+    there = [following(cycles, spot) == MEET["eo".index(spot[1])] for cycles in TO_ROOT]
+    return 1 + there.index(True) if True in there else 0
+
+
+def carried(k):
+    ends = [following((BACK + (SWAP,))[k], root) for root in MEET]
+    return [block_of(end) if end[1] == "eo"[p] else 0 for p, end in enumerate(ends)]
+
+
+def turn_of(spot):
+    root = MEET["eo".index(spot[1])]
     back = [following(cycles, root) == spot for cycles in BACK + (SWAP,)]
-    block = 1 + there.index(True) if True in there else 0
-    source = 1 + back.index(True) if spot != root else 0
-    return source * PLACES + block
+    return 1 + back.index(True) if spot != root else 0
 
 
 def pairs(cycles, batches):
@@ -112,7 +119,7 @@
     scores[...] = pair_scores(normed[...], normed[...])
 
 
-def late_body(normed, scores, guest, own_ids, other_ids, early_id, id1, id2, raw1, raw2, out):
+def late_body(normed, scores, guest, own_ids, other_ids, early_id, id1, id2, raw1, raw2, own, *backs):
     count, half = raw1.shape[0], normed.shape[0]
     first = jnp.where(guest[...] > 0, other_ids[...], own_ids[...])
     early_row = jnp.concatenate([first, early_id[...]], axis=1)
@@ -130,10 +137,14 @@
     across = jnp.max(jnp.transpose(across), axis=0, keepdims=True)
     early_best = best_of(scores[...], (early_column == early_row) & apart)
     early_best = jnp.maximum(early_best, across)
-    for k, best in enumerate((early_best, late_best)):
+    blocks = []
+    for best in (early_best, late_best):
         best = jnp.maximum(best, -1.0)
-        out[2 * k : 2 * k + 1, :] = best[:, :count]
-        out[2 * k + 1 : 2 * k + 2, :] = best[:, count:]
+        blocks += [best[:, :count], best[:, count:]]
+    own[...] = blocks[0]
+    for k, back in enumerate(backs):
+        even, odd = carried(k)
+        back[...] = jnp.where(guest[...] > 0, blocks[even], blocks[odd])
 
 
 def own_rows(rows):
@@ -165,9 +176,9 @@
 def all_results(*args):
     return pl.pallas_call(
         late_body,
-        out_shape=jax.ShapeDtypeStruct((PLACES, args[-1].shape[0]), jnp.float32),
+        out_shape=(jax.ShapeDtypeStruct((1, args[-1].shape[0]), jnp.float32),) * (1 + PLACES),
         in_specs=[WHOLE] * len(args),
-        out_specs=WHOLE,
+        out_specs=(WHOLE,) * (1 + PLACES),
         compiler_params=GRANT,
         name="all_results",
     )(*args)
@@ -182,21 +193,20 @@
         where_am_i = lax.axis_index(SPAN) * 2 + (lax.axis_index(BATCH) & 1)
         guest = where_am_i == int(MEET[0][0]) * 2 + "eo".index(MEET[0][1])
         guest = jnp.broadcast_to(guest.astype(jnp.int32), cluster_ids.shape)
+        turn = jnp.zeros(cluster_ids.shape, jnp.int32)
+        for code in range(PLACES * 2):
+            spot = f"{code // 2}{'eo'[code % 2]}"
+            turn = jnp.where(where_am_i == code, turn_of(spot), turn)
         inward, outward = TO_ROOT + (SWAP,), BACK + (SWAP,)
         arrived = [travel(rows, c, batches) for c in inward]
         arrived_ids = [travel(cluster_ids, c, batches) for c in inward]
         normed, scores = early_pairs(guest, own_rows(rows), arrived[-1], arrived[0])
         ids = [guest, cluster_ids, arrived_ids[-1]] + arrived_ids[:-1]
-        best = all_results(normed, scores, *ids, *arrived[1:-1])
-        back = [travel(best, c, batches) for c in outward]
-        stack = jnp.concatenate([best] + back, axis=0)
-        row = lax.broadcasted_iota(jnp.int32, stack.shape, 0)
-        mine = jnp.zeros(stack.shape, jnp.bool_)
-        for place in range(PLACES):
-            for parity in range(2):
-                here = where_am_i == place * 2 + parity
-                mine |= here & (row == wanted(place, parity))
-        return jnp.max(jnp.where(mine, stack, -1.0), axis=0)[None, :]
+        result, *sent = all_results(normed, scores, *ids, *arrived[1:-1])
+        for k, cycles in enumerate(outward):
+            back = travel(sent[k], cycles, batches)
+            result = jnp.where(turn == k + 1, back, result)
+        return result
 
     return per_device
 

time: 17.6 us -> 18.1 us (1.028)
  starting transfers between devices: 12.4 us -> 13.1 us
    ppermute x12, starting transfers between devices: 12.4 us -> 13.1 us  [travel(): return lax.ppermute(array, (SPAN, BATCH), pairs(cycles, batches))]
    reduce_max x1 -> x0, other arithmetic: 0.6 us -> none  [whole(): return jnp.max(jnp.where(mine, stack, -1.0), axis=0)[None, :]]
    select_n x0 -> x1, other arithmetic: none -> 0.51 us  [whole(): result = jnp.where(turn == k + 1, back, result)]
where the time goes in v4:
time: 18.1 us; the launch traced here: 18 us
  starting transfers between devices  13.1 us (72%)
  waiting for transfers between devices  2.16 us (12%)
  Pallas kernels  1.19 us (7%)
  local copies, waits for them, and re-layouts  0.93 us (5%)
  other arithmetic  0.51 us (3%)
    ppermute x12, starting transfers between devices, travel(): return lax.ppermute(array, (SPAN, BATCH), pairs(cycles, batches))  13.1 us
    ppermute x12, waiting for transfers between devices, travel(): return lax.ppermute(array, (SPAN, BATCH), pairs(cycles, batches))  2.16 us
    unnamed x4, local copies, waits for them, and re-layouts  0.93 us
    pallas_call x1, Pallas kernels, all_results(): pl.pallas_call(late_body, out_shape=(jax.ShapeDtypeStruct((1, args[-1].sh...  0.59 us
    select_n x1, other arithmetic, whole(): result = jnp.where(turn == k + 1, back, result)  0.51 us
    pallas_call x1, Pallas kernels, early_pairs(): pl.pallas_call(early_body, out_shape=(jax.ShapeDtypeStruct((rows, width),...  0.47 us
  transfers between devices with their start and end apart: 12, of which 3 were waited for; matrix products, arithmetic and copies ran while one was open for 0% of the time, Pallas kernels for 3%

profile of v4, /device:TPU:0, one launch (start us, length us, event | category | flops | bytes accessed | tf_op | source)
XLA Modules:
  0.0 18.0 jit_solution(9092210012202141593)
XLA Ops:
  0.0 0.5 %collective-permute-start = (bf16[128,768]{1,0:T(8,128)(2,1)}, bf16[128,768]{1,0:T(8,128)(2,1)S(1)}, u32[]{:S(2)}, u32[]{:S(2)}) collective-permute-start(bf16[128,768]{1,0:T(8,128)(2,1)} %bitcast.1), channel_id=1, source_target_pairs={{0,1},{1,0},{2,3},{3,2},{4,5},{5,4},{6,7},{7,6},{8,9},{9,8},{10,11... | collective-permute-start | bytes 589832 | tf_op jit(solution)/shard_map/ppermute | solution.py:95
  0.5 0.1 collective-permute-start.1
  0.6 3.7 %collective-permute-start.6 = (bf16[128,768]{1,0:T(8,128)(2,1)}, bf16[128,768]{1,0:T(8,128)(2,1)S(1)}, u32[]{:S(2)}, u32[]{:S(2)}) collective-permute-start(bf16[128,768]{1,0:T(8,128)(2,1)} %bitcast.3), channel_id=1, source_target_pairs={{0,1},{1,0},{2,3},{3,2},{4,6},{5,9},{6,4},{7,11},{8,5},{9,8},{10,7... | collective-permute-start | bytes 589832 | tf_op jit(solution)/shard_map/ppermute | solution.py:95
  4.3 0.2 %collective-permute-start.7 = (bf16[128,768]{1,0:T(8,128)(2,1)}, bf16[128,768]{1,0:T(8,128)(2,1)S(1)}, u32[]{:S(2)}, u32[]{:S(2)}) collective-permute-start(bf16[128,768]{1,0:T(8,128)(2,1)} %bitcast.4), channel_id=1, source_target_pairs={{0,5},{1,0},{2,7},{3,2},{4,1},{5,4},{6,3},{7,6},{8,13},{9,8},{10,1... | collective-permute-start | bytes 589832 | tf_op jit(solution)/shard_map/ppermute | solution.py:95
  4.5 0.3 %collective-permute-start.2 = (s32[1,128]{1,0:T(1,128)S(1)}, s32[1,128]{1,0:T(1,128)S(1)}, u32[]{:S(2)}, u32[]{:S(2)}) collective-permute-start(s32[1,128]{1,0:T(1,128)S(1)} %copy-done.1), channel_id=1, source_target_pairs={{0,1},{1,0},{2,3},{3,2},{4,5},{5,4},{6,7},{7,6},{8,9},{9,8},{10,11... | collective-permute-start | bytes 1544 | tf_op jit(solution)/shard_map/ppermute | solution.py:95
  4.8 0.9 %copy-done = bf16[1,128,768]{2,1,0:T(8,128)(2,1)S(1)} copy-done((bf16[1,128,768]{2,1,0:T(8,128)(2,1)S(1)}, bf16[1,128,768]{2,1,0:T(8,128)(2,1)}, u32[]{:S(2)}) %copy-start) | copy-done | bytes 196632
  5.7 0.1 own_rows.1.own
  5.9 0.1 collective-permute-done.2.other_ids
  6.0 0.2 %collective-permute-start.3 = (s32[1,128]{1,0:T(1,128)S(1)}, s32[1,128]{1,0:T(1,128)S(1)}, u32[]{:S(2)}, u32[]{:S(2)}) collective-permute-start(s32[1,128]{1,0:T(1,128)S(1)} %copy-done.1), channel_id=1, source_target_pairs={{0,1},{1,9},{2,3},{3,11},{4,0},{5,4},{6,2},{7,6},{8,13},{9,8},{10,... | collective-permute-start | bytes 1544 | tf_op jit(solution)/shard_map/ppermute | solution.py:95
  6.2 0.0 collective-permute-done.other
  6.2 1.4 %collective-permute-start.4 = (s32[1,128]{1,0:T(1,128)S(1)}, s32[1,128]{1,0:T(1,128)S(1)}, u32[]{:S(2)}, u32[]{:S(2)}) collective-permute-start(s32[1,128]{1,0:T(1,128)S(1)} %copy-done.1), channel_id=1, source_target_pairs={{0,1},{1,0},{2,3},{3,2},{4,6},{5,9},{6,4},{7,11},{8,5},{9,8},{10,7... | collective-permute-start | bytes 1544 | tf_op jit(solution)/shard_map/ppermute | solution.py:95
  7.6 0.0 collective-permute-done.1.raw
  7.6 2.6 %collective-permute-start.5 = (s32[1,128]{1,0:T(1,128)S(1)}, s32[1,128]{1,0:T(1,128)S(1)}, u32[]{:S(2)}, u32[]{:S(2)}) collective-permute-start(s32[1,128]{1,0:T(1,128)S(1)} %copy-done.1), channel_id=1, source_target_pairs={{0,5},{1,0},{2,7},{3,2},{4,1},{5,4},{6,3},{7,6},{8,13},{9,8},{10,1... | collective-permute-start | bytes 1544 | tf_op jit(solution)/shard_map/ppermute | solution.py:95
  10.2 0.5 %early_pairs.1 = (bf16[256,768]{1,0:T(8,128)(2,1)S(1)}, f32[256,256]{1,0:T(8,128)S(1)}) custom-call(s32[1,128]{1,0:T(1,128)S(1)} %broadcast_in_dim.22.guest, bf16[128,768]{1,0:T(8,128)(2,1)S(1)} %own_rows.1.own, bf16[128,768]{1,0:T(8,128)(2,1)S(1)} %collective-permute-done.other, bf16[128,768]{1,0:T(8,128)(2,1)S(1)} %collective-permute-done.1.raw), custom_call_target="tpu_custom_call" | custom-call | tf_op jit(solution)/shard_map/early_pairs/pallas_call | solution.py:163
  10.7 0.0 collective-permute-done.3.early_id
  10.7 0.0 collective-permute-done.4.id1
  10.7 0.8 %collective-permute-done.5.id2 = s32[1,128]{1,0:T(1,128)S(1)} collective-permute-done((s32[1,128]{1,0:T(1,128)S(1)}, s32[1,128]{1,0:T(1,128)S(1)}, u32[]{:S(2)}, u32[]{:S(2)}) %collective-permute-start.5) | collective-permute-done | bytes 544 | tf_op jit(solution)/shard_map/ppermute | solution.py:95
  11.6 0.6 %all_results.1 = (f32[1,128]{1,0:T(1,128)S(1)}, f32[1,128]{1,0:T(1,128)S(1)}, f32[1,128]{1,0:T(1,128)S(1)}, f32[1,128]{1,0:T(1,128)S(1)}, f32[1,128]{1,0:T(1,128)S(1)}) custom-call(bf16[256,768]{1,0:T(8,128)(2,1)S(1)} %get-tuple-element.12.normed, f32[256,256]{1,0:T(8,128)S(1)} %get-tuple-element.13.scores, s32[1,128]{1,0:T(1,128)S(1)} %broadcast_in_dim.22.guest, ...), custom_call_target="tpu_custom_call" | custom-call | tf_op jit(solution)/shard_map/all_results/pallas_call | solution.py:177
  12.1 0.1 collective-permute-start.8
  12.2 0.5 %collective-permute-start.9 = (f32[1,128]{1,0:T(1,128)S(1)}, f32[1,128]{1,0:T(1,128)S(1)}, u32[]{:S(2)}, u32[]{:S(2)}) collective-permute-start(f32[1,128]{1,0:T(1,128)S(1)} %get-tuple-element.15), channel_id=1, source_target_pairs={{0,1},{1,0},{2,3},{3,2},{4,9},{5,12},{6,11},{7,14},{8,4},{9,5},{10... | collective-permute-start | bytes 1544 | tf_op jit(solution)/shard_map/ppermute | solution.py:95
  12.7 0.1 collective-permute-start.10
  12.8 3.4 %collective-permute-start.11 = (f32[1,128]{1,0:T(1,128)S(1)}, f32[1,128]{1,0:T(1,128)S(1)}, u32[]{:S(2)}, u32[]{:S(2)}) collective-permute-start(f32[1,128]{1,0:T(1,128)S(1)} %get-tuple-element.17), channel_id=1, source_target_pairs={{0,8},{1,4},{2,10},{3,6},{4,5},{5,0},{6,7},{7,2},{8,9},{9,1},{10,1... | collective-permute-start | bytes 1544 | tf_op jit(solution)/shard_map/ppermute | solution.py:95
  16.2 1.3 %collective-permute-done.11 = f32[1,128]{1,0:T(1,128)S(1)} collective-permute-done((f32[1,128]{1,0:T(1,128)S(1)}, f32[1,128]{1,0:T(1,128)S(1)}, u32[]{:S(2)}, u32[]{:S(2)}) %collective-permute-start.11) | collective-permute-done | bytes 544 | tf_op jit(solution)/shard_map/ppermute | solution.py:95
  17.5 0.5 %broadcast_select_fusion.3 = f32[1,128]{1,0:T(1,128)} fusion(f32[1,128]{1,0:T(1,128)S(1)} %collective-permute-done.8, pred[]{:T(512)S(6)} %eq.61, f32[1,128]{1,0:T(1,128)S(1)} %collective-permute-done.9, pred[]{:T(512)S(6)} %eq.62, f32[1,128]{1,0:T(1,128)S(1)} %collective-permute-done.10, pred[]{:T(512)S(6)} %eq.63, f32[1,128]{1,0:T(1,128)S(1)} %collective-permute-done.11, ...), kind=kLoop, calls=%fused_computation.3 | loop fusion | flops 512 | bytes 3076 | tf_op jit(solution)/shard_map/jit(_where)/select_n | solution.py:208
  (9 shorter events, 0.0 us)
Async XLA Ops:
  0.0 4.5 %copy-start.1 = (s32[1,128]{1,0:T(1,128)S(1)}, s32[1,128]{1,0:T(1,128)}, u32[]{:S(2)}) copy-start(s32[1,128]{1,0:T(1,128)} %own_ids.1) | copy-start | bytes 1540
  0.0 6.2 %collective-permute-start = (bf16[128,768]{1,0:T(8,128)(2,1)}, bf16[128,768]{1,0:T(8,128)(2,1)S(1)}, u32[]{:S(2)}, u32[]{:S(2)}) collective-permute-start(bf16[128,768]{1,0:T(8,128)(2,1)} %bitcast.1), channel_id=1, source_target_pairs={{0,1},{1,0},{2,3},{3,2},{4,5},{5,4},{6,7},{7,6},{8,9},{9,8},{10,11... | collective-permute-start | bytes 589832 | tf_op jit(solution)/shard_map/ppermute | solution.py:95
  0.5 7.1 %collective-permute-start.1 = (bf16[128,768]{1,0:T(8,128)(2,1)}, bf16[128,768]{1,0:T(8,128)(2,1)S(1)}, u32[]{:S(2)}, u32[]{:S(2)}) collective-permute-start(bf16[128,768]{1,0:T(8,128)(2,1)} %bitcast.2), channel_id=1, source_target_pairs={{0,1},{1,9},{2,3},{3,11},{4,0},{5,4},{6,2},{7,6},{8,13},{9,8},{10,... | collective-permute-start | bytes 589832 | tf_op jit(solution)/shard_map/ppermute | solution.py:95
  0.6 11.0 %collective-permute-start.6 = (bf16[128,768]{1,0:T(8,128)(2,1)}, bf16[128,768]{1,0:T(8,128)(2,1)S(1)}, u32[]{:S(2)}, u32[]{:S(2)}) collective-permute-start(bf16[128,768]{1,0:T(8,128)(2,1)} %bitcast.3), channel_id=1, source_target_pairs={{0,1},{1,0},{2,3},{3,2},{4,6},{5,9},{6,4},{7,11},{8,5},{9,8},{10,7... | collective-permute-start | bytes 589832 | tf_op jit(solution)/shard_map/ppermute | solution.py:95
  4.3 7.3 %collective-permute-start.7 = (bf16[128,768]{1,0:T(8,128)(2,1)}, bf16[128,768]{1,0:T(8,128)(2,1)S(1)}, u32[]{:S(2)}, u32[]{:S(2)}) collective-permute-start(bf16[128,768]{1,0:T(8,128)(2,1)} %bitcast.4), channel_id=1, source_target_pairs={{0,5},{1,0},{2,7},{3,2},{4,1},{5,4},{6,3},{7,6},{8,13},{9,8},{10,1... | collective-permute-start | bytes 589832 | tf_op jit(solution)/shard_map/ppermute | solution.py:95
  4.5 1.4 %collective-permute-start.2 = (s32[1,128]{1,0:T(1,128)S(1)}, s32[1,128]{1,0:T(1,128)S(1)}, u32[]{:S(2)}, u32[]{:S(2)}) collective-permute-start(s32[1,128]{1,0:T(1,128)S(1)} %copy-done.1), channel_id=1, source_target_pairs={{0,1},{1,0},{2,3},{3,2},{4,5},{5,4},{6,7},{7,6},{8,9},{9,8},{10,11... | collective-permute-start | bytes 1544 | tf_op jit(solution)/shard_map/ppermute | solution.py:95
  4.8 0.9 %copy-start = (bf16[1,128,768]{2,1,0:T(8,128)(2,1)S(1)}, bf16[1,128,768]{2,1,0:T(8,128)(2,1)}, u32[]{:S(2)}) copy-start(bf16[1,128,768]{2,1,0:T(8,128)(2,1)} %param.2) | copy-start | bytes 589828
  6.0 4.8 %collective-permute-start.3 = (s32[1,128]{1,0:T(1,128)S(1)}, s32[1,128]{1,0:T(1,128)S(1)}, u32[]{:S(2)}, u32[]{:S(2)}) collective-permute-start(s32[1,128]{1,0:T(1,128)S(1)} %copy-done.1), channel_id=1, source_target_pairs={{0,1},{1,9},{2,3},{3,11},{4,0},{5,4},{6,2},{7,6},{8,13},{9,8},{10,... | collective-permute-start | bytes 1544 | tf_op jit(solution)/shard_map/ppermute | solution.py:95
  6.2 4.5 %collective-permute-start.4 = (s32[1,128]{1,0:T(1,128)S(1)}, s32[1,128]{1,0:T(1,128)S(1)}, u32[]{:S(2)}, u32[]{:S(2)}) collective-permute-start(s32[1,128]{1,0:T(1,128)S(1)} %copy-done.1), channel_id=1, source_target_pairs={{0,1},{1,0},{2,3},{3,2},{4,6},{5,9},{6,4},{7,11},{8,5},{9,8},{10,7... | collective-permute-start | bytes 1544 | tf_op jit(solution)/shard_map/ppermute | solution.py:95
  7.6 3.9 %collective-permute-start.5 = (s32[1,128]{1,0:T(1,128)S(1)}, s32[1,128]{1,0:T(1,128)S(1)}, u32[]{:S(2)}, u32[]{:S(2)}) collective-permute-start(s32[1,128]{1,0:T(1,128)S(1)} %copy-done.1), channel_id=1, source_target_pairs={{0,5},{1,0},{2,7},{3,2},{4,1},{5,4},{6,3},{7,6},{8,13},{9,8},{10,1... | collective-permute-start | bytes 1544 | tf_op jit(solution)/shard_map/ppermute | solution.py:95
  12.1 4.0 %collective-permute-start.8 = (f32[1,128]{1,0:T(1,128)S(1)}, f32[1,128]{1,0:T(1,128)S(1)}, u32[]{:S(2)}, u32[]{:S(2)}) collective-permute-start(f32[1,128]{1,0:T(1,128)S(1)} %get-tuple-element.14), channel_id=1, source_target_pairs={{0,1},{1,0},{2,3},{3,2},{4,5},{5,4},{6,7},{7,6},{8,9},{9,8},{10,11... | collective-permute-start | bytes 1544 | tf_op jit(solution)/shard_map/ppermute | solution.py:95
  12.2 4.0 %collective-permute-start.9 = (f32[1,128]{1,0:T(1,128)S(1)}, f32[1,128]{1,0:T(1,128)S(1)}, u32[]{:S(2)}, u32[]{:S(2)}) collective-permute-start(f32[1,128]{1,0:T(1,128)S(1)} %get-tuple-element.15), channel_id=1, source_target_pairs={{0,1},{1,0},{2,3},{3,2},{4,9},{5,12},{6,11},{7,14},{8,4},{9,5},{10... | collective-permute-start | bytes 1544 | tf_op jit(solution)/shard_map/ppermute | solution.py:95
  12.7 3.5 %collective-permute-start.10 = (f32[1,128]{1,0:T(1,128)S(1)}, f32[1,128]{1,0:T(1,128)S(1)}, u32[]{:S(2)}, u32[]{:S(2)}) collective-permute-start(f32[1,128]{1,0:T(1,128)S(1)} %get-tuple-element.16), channel_id=1, source_target_pairs={{0,1},{1,0},{2,3},{3,2},{4,5},{5,8},{6,7},{7,10},{8,4},{9,13},{10,... | collective-permute-start | bytes 1544 | tf_op jit(solution)/shard_map/ppermute | solution.py:95
  12.8 4.7 %collective-permute-start.11 = (f32[1,128]{1,0:T(1,128)S(1)}, f32[1,128]{1,0:T(1,128)S(1)}, u32[]{:S(2)}, u32[]{:S(2)}) collective-permute-start(f32[1,128]{1,0:T(1,128)S(1)} %get-tuple-element.17), channel_id=1, source_target_pairs={{0,8},{1,4},{2,10},{3,6},{4,5},{5,0},{6,7},{7,2},{8,9},{9,1},{10,1... | collective-permute-start | bytes 1544 | tf_op jit(solution)/shard_map/ppermute | solution.py:95
